TPU v7x, 32 devices: a whole 2x2x4 slice. The times are simulated.
32 devices in a mesh: ens: 2 (over x), lat: 16 (over z, y, core).
Axes of the slice: x: 2, y: 2, z: 4, core: 2. Of those that a mesh axis runs over, the one named last changes fastest.
Arguments:
- atmos: bfloat16 [11520, 1024], P(('ens', 'lat')), parts along dimension 0, may hold values from -6 to 6
- ocean_state: bfloat16 [76, 128, 1440], P(None, ('ens', 'lat')), parts along dimension 1, may hold values from -6 to 6
- land_mask: int32 [64, 1440], P('lat'), may hold values 0 or 1
- w_qkv: bfloat16 [1024, 3072], replicated, may hold values from -0.1875 to 0.1875
- w_out: bfloat16 [1024, 1024], replicated, may hold values from -0.1875 to 0.1875
- head_scale: float32 [16], replicated, may hold values from 0.5 to 80
- gain_attn: float32 [1024], replicated, may hold values from 0.5 to 1.5
- gain_flux: float32 [1024], replicated, may hold values from 0.1 to 1.9
- w_flux: bfloat16 [1024, 16], replicated, may hold values from -0.1875 to 0.1875
- surf_embed: float32 [4, 1024], replicated, may hold values from -3 to 3
- flux_start: int32 [64], P('lat'), may hold values from 0 to 14, as said below
- flux_weight: float32 [64, 2], P('lat'), may hold values from 0.25 to 1
- surf_start: int32 [16], P('lat'), may hold values from -2 to 59, as said below
- surf_weight: float32 [16, 7], P('lat'), may hold values from 0.1 to 0.5
- conv_first: bfloat16 [9, 128, 92], replicated, may hold values from -0.21875 to 0.21875
- conv_second: bfloat16 [9, 76, 128], replicated, may hold values from -0.1875 to 0.1875
Outputs:
- atmos_next: bfloat16 [11520, 1024], P(('ens', 'lat')), parts along dimension 0
- ocean_next: bfloat16 [76, 128, 1440], P(None, ('ens', 'lat')), parts along dimension 1
There are 2 independent parts, one for each index of `ens`. A program takes and returns all parts, laid end to end along the dimension named above; an argument that names none is the same for every part. Nothing has to cross between parts.
Inputs may be any that keep to these rules, and one draw needn't show every extreme that they name: flux_start[i] is i // 4 - 1 or i // 4, kept within 0 to 14. surf_start[r] is 4 r - 2 or 4 r - 1.
All inputs are finite; a program needn't handle non-finite values. No bound on the sum of `land_mask` on one device may be relied on, other than what follows from the above.
Results may differ from a plain program's by a relative error of at most 0.0065.
The roundings to bfloat16 on the way count: a program that leaves them out, or rounds other values in their place, can miss the bound.
Values may be sent and summed in bfloat16 or wider, within the bound.
A program may use at most 128 MiB of HBM per device.

v0:
```python
import jax
import jax.numpy as jnp
from jax import lax
from jax.experimental import pallas as pl
from jax.experimental.pallas import tpu as pltpu
from jax.sharding import PartitionSpec as P

LEVELS = 19
VARS = 4
SPAN = 4
OSTEPS = 2


def padded_2(block, sides, width):
    for axis, dim in sides:
        count = lax.axis_size(axis)
        forward = [(i, i + 1) for i in range(count - 1)]
        backward = [(target, source) for source, target in forward]
        low = lax.ppermute(
            lax.slice_in_dim(block, block.shape[dim] - width, None, axis=dim), axis, forward
        )
        high = lax.ppermute(lax.slice_in_dim(block, 0, width, axis=dim), axis, backward)
        block = jnp.concatenate([low, block, high], axis=dim)
    return block


def rms_norm(values, scaling):
    return values * lax.rsqrt(jnp.mean(values * values, axis=-1, keepdims=True) + 1e-06) * scaling


def band_matrix(starts, weight, first_col, col_count):
    columns = first_col + jnp.arange(col_count, dtype=jnp.int32)
    summed = jnp.zeros((starts.shape[0], col_count), jnp.float32)
    for offset in range(weight.shape[1]):
        matches = (columns[None, :] == starts[:, None] + offset).astype(jnp.float32)
        summed = summed + weight[:, offset : offset + 1] * matches
    return summed


def surface_rows(ocean_now):
    fields = ocean_now[0::LEVELS]
    averaged = jnp.mean(
        fields.reshape(fields.shape[0], fields.shape[1], fields.shape[2] // SPAN, SPAN), axis=3
    )
    return averaged.transpose(1, 0, 2).reshape(fields.shape[1], -1)


def norm_keys(key_raw, head_count):
    token_count = key_raw.shape[0]
    shaped = key_raw.reshape(token_count, head_count, -1)
    normed = shaped * lax.rsqrt(jnp.mean(shaped * shaped, axis=-1, keepdims=True) + 1e-06)
    return normed.astype(jnp.bfloat16).reshape(token_count, -1)


def attend(query_rows, key_rows, value_rows, valid):
    key_count = key_rows.shape[0]
    scores = jnp.einsum("qhd,khd->hqk", query_rows, key_rows, preferred_element_type=jnp.float32)
    scores = jnp.where(valid[None, None, :], scores, -1e30)
    largest = jnp.max(scores, axis=2, keepdims=True)
    raised = jnp.exp(scores - largest)
    probs = (raised / jnp.sum(raised, axis=2, keepdims=True)).astype(jnp.bfloat16)
    value_heads = value_rows.reshape(key_count, key_rows.shape[1], key_rows.shape[2])
    mixed = jnp.einsum("hqk,khd->qhd", probs, value_heads, preferred_element_type=jnp.float32)
    return mixed.astype(jnp.bfloat16).reshape(query_rows.shape[0], -1)


def ocean_kernel(pos_ref, mat_ref, low_ref, mid_ref, high_ref, mask_ref, flux_ref, spread_ref,
                 first_ref, second_ref, out_ref, xs, hs, st):
    och = mid_ref.shape[1]
    olon = mid_ref.shape[2]
    orows = mid_ref.shape[0]
    wide = xs.shape[1]
    nflux = flux_ref.shape[1]
    spread_rows = flux_ref.shape[0]
    hid = first_ref.shape[0] // 3
    opad = second_ref.shape[0] // 3
    stride = opad + nflux
    first_row = pos_ref[0]
    total = pos_ref[1]
    tail = wide - 128
    first_pad = olon - tail

    def wrap(head, last):
        lane = lax.broadcasted_iota(jnp.int32, last.shape, 1)
        end = pltpu.roll(last, 128 - first_pad, 1)
        begin = pltpu.roll(head, first_pad, 1)
        return jnp.where(lane == first_pad, begin, jnp.where(lane == 127, end, last))

    def combine(full, size):
        left = pltpu.roll(full[0:size], 1, 1)
        right = pltpu.roll(full[2 * size : 3 * size], wide - 1, 1)
        return left + full[size : 2 * size] + right

    for part, ref in enumerate((low_ref, mid_ref, high_ref)):
        def fill(i, carry, ref=ref, part=part):
            row = part * orows + i
            state = ref[i].astype(jnp.float32)
            state = jnp.concatenate([state, jnp.zeros((opad - och, olon), jnp.float32)], axis=0)
            last = jnp.concatenate(
                [state[:, tail:], jnp.zeros((opad, wide - olon), jnp.float32)], axis=1
            )
            st[row, :, 0:tail] = state[:, 0:tail]
            st[row, :, tail:] = wrap(state[:, 0:128], last)
            base = pl.multiple_of(row * stride, 16)
            xs[pl.ds(base, opad), :] = st[row].astype(jnp.bfloat16)
            return carry
        lax.fori_loop(0, orows, fill, 0)

    def regrid(row, carry):
        total_flux = mat_ref[row, 0] * flux_ref[0].astype(jnp.float32)
        for r in range(1, spread_rows):
            total_flux = total_flux + mat_ref[row, r] * flux_ref[r].astype(jnp.float32)
        rows = jnp.dot(total_flux.astype(jnp.bfloat16), spread_ref[...],
                       preferred_element_type=jnp.float32)
        base = pl.multiple_of(row * stride + opad, 16)
        xs[pl.ds(base, nflux), :] = rows.astype(jnp.bfloat16)
        return carry
    lax.fori_loop(0, 3 * orows, regrid, 0)

    for step in range(OSTEPS):
        edge = 1 + 2 * step

        def first(row, carry):
            block = xs[pl.ds(pl.multiple_of((row - 1) * stride, 16), 3 * stride), :]
            full = jnp.dot(first_ref[...], block, preferred_element_type=jnp.float32)
            hidden = jax.nn.gelu(combine(full, hid), approximate=True)
            place = first_row + row - orows
            inside = jnp.where((place >= 0) & (place < total), 1.0, 0.0).astype(jnp.float32)
            hidden = hidden * inside
            base = pl.multiple_of(row * hid, 16)
            hs[pl.ds(base, hid), 0:tail] = hidden[:, 0:tail].astype(jnp.bfloat16)
            hs[pl.ds(base, hid), tail:] = wrap(hidden[:, 0:128], hidden[:, tail:]).astype(jnp.bfloat16)
            return carry
        lax.fori_loop(edge, 3 * orows - edge, first, 0)

        def second(row, carry):
            block = hs[pl.ds(pl.multiple_of((row - 1) * hid, 16), 3 * hid), :]
            full = jnp.dot(second_ref[...], block, preferred_element_type=jnp.float32)
            state = st[row] + mask_ref[row] * combine(full, opad)
            if step == OSTEPS - 1:
                out_ref[row - orows] = state[0:och, 0:olon].astype(jnp.bfloat16)
            else:
                st[row, :, 0:tail] = state[:, 0:tail]
                st[row, :, tail:] = wrap(state[:, 0:128], state[:, tail:])
                base = pl.multiple_of(row * stride, 16)
                xs[pl.ds(base, opad), :] = st[row].astype(jnp.bfloat16)
            return carry
        lax.fori_loop(edge + 1, 3 * orows - edge - 1, second, 0)


def round_up(value, unit):
    return (value + unit - 1) // unit * unit


def ocean_steps(state_parts, mask, fluxes, matrix, conv_first, conv_second, position, band_count):
    orows, och, olon = state_parts[1].shape
    nflux = fluxes.shape[1]
    hid = conv_first.shape[1]
    opad = round_up(och, 16)
    wide = round_up(olon + 2, 128)
    alon = fluxes.shape[2]
    first = conv_first.reshape(3, 3, hid, och + nflux)
    first = jnp.concatenate(
        [first[..., :och], jnp.zeros((3, 3, hid, opad - och), first.dtype), first[..., och:]], axis=3
    )
    first = first.transpose(1, 2, 0, 3).reshape(3 * hid, 3 * (opad + nflux))
    second = jnp.pad(conv_second.reshape(3, 3, och, hid), ((0, 0), (0, 0), (0, opad - och), (0, 0)))
    second = second.transpose(1, 2, 0, 3).reshape(3 * opad, 3 * hid)
    column = jnp.arange(wide, dtype=jnp.int32)
    longitude = jnp.where(column < olon, column, jnp.where(column == olon, 0, olon - 1))
    spread = (longitude[None, :] // SPAN == jnp.arange(alon, dtype=jnp.int32)[:, None]).astype(jnp.bfloat16)
    scalars = jnp.stack([position * orows, band_count * orows]).astype(jnp.int32)
    mask = jnp.pad(mask.astype(jnp.float32), ((0, 0), (0, wide - olon)))[:, None, :]
    vmem = pl.BlockSpec(memory_space=pltpu.VMEM)
    smem = pl.BlockSpec(memory_space=pltpu.SMEM)
    return pl.pallas_call(
        ocean_kernel,
        out_shape=jax.ShapeDtypeStruct((orows, och, olon), jnp.bfloat16),
        in_specs=[smem, smem] + [vmem] * 8,
        out_specs=vmem,
        scratch_shapes=[
            pltpu.VMEM((3 * orows * (opad + nflux), wide), jnp.bfloat16),
            pltpu.VMEM((3 * orows * hid, wide), jnp.bfloat16),
            pltpu.VMEM((3 * orows, opad, wide), jnp.float32),
        ],
        compiler_params=pltpu.CompilerParams(vmem_limit_bytes=60 * 1024 * 1024),
        name="ocean_steps",
    )(scalars, matrix, *state_parts, mask, fluxes, spread, first, second)


def shifted(block, offset):
    count = lax.axis_size("lat")
    pairs = [(i, i + offset) for i in range(count) if 0 <= i + offset < count]
    return lax.ppermute(block, "lat", pairs)


def local(
    atmos,
    ocean_state,
    land_mask,
    w_qkv,
    w_out,
    head_scale,
    gain_attn,
    gain_flux,
    w_flux,
    surf_embed,
    flux_start,
    flux_weight,
    surf_start,
    surf_weight,
    conv_first,
    conv_second,
):
    position = lax.axis_index("lat")
    band_count = lax.axis_size("lat")
    ocean_now = ocean_state.astype(jnp.float32)
    orows = ocean_now.shape[1]
    olon = ocean_now.shape[2]
    alon = olon // SPAN
    arows = atmos.shape[0] // alon
    width = atmos.shape[1]
    head_count = head_scale.shape[0]
    depth = width // head_count
    flux_count = w_flux.shape[1]
    surface = surface_rows(ocean_now).astype(jnp.bfloat16)
    surf_near = padded_2(surface, (("lat", 0),), 2)
    surf_matrix = band_matrix(surf_start, surf_weight, position * orows - 2, orows + 4)
    surf_atm = jnp.dot(surf_matrix, surf_near.astype(jnp.float32), precision=lax.Precision.HIGHEST)
    surf_tokens = surf_atm.reshape(arows, VARS, alon).transpose(0, 2, 1).reshape(arows * alon, VARS)
    start = atmos.astype(jnp.float32) + jnp.dot(
        surf_tokens, surf_embed, precision=lax.Precision.HIGHEST
    )
    normed = rms_norm(start, gain_attn).astype(jnp.bfloat16)
    qkv = jnp.dot(normed, w_qkv, preferred_element_type=jnp.float32)
    token_count = qkv.shape[0]
    query_raw = qkv[:, :width].reshape(token_count, head_count, depth)
    query_part = query_raw * lax.rsqrt(
        jnp.mean(query_raw * query_raw, axis=-1, keepdims=True) + 1e-06
    )
    query_part = (query_part * (head_scale[None, :, None] / jnp.sqrt(jnp.float32(depth)))).astype(
        jnp.bfloat16
    )
    key_part = norm_keys(qkv[:, width : 2 * width], head_count)
    value_part = qkv[:, 2 * width :].astype(jnp.bfloat16)
    key_ext, value_ext = (
        padded_2(key_part, (("lat", 0),), alon),
        padded_2(value_part, (("lat", 0),), alon),
    )
    key_rows = key_ext.reshape(3 * alon, head_count, depth)
    global_rows = position * arows + 0 - 1 + jnp.arange(3 * alon, dtype=jnp.int32) // alon
    valid = (global_rows >= 0) & (global_rows < arows * band_count)
    pieces = attend(query_part, key_rows, value_ext, valid)
    after = start + jnp.dot(pieces, w_out, preferred_element_type=jnp.float32)
    atmos_next = after.astype(jnp.bfloat16)
    flux_in = rms_norm(after, gain_flux).astype(jnp.bfloat16)
    fluxes = jnp.einsum(
        "td,df->ft", flux_in, w_flux, preferred_element_type=jnp.float32
    ).astype(jnp.bfloat16)[None]
    flux_rows = jnp.concatenate(
        [shifted(fluxes, 2), shifted(fluxes, 1), fluxes, shifted(fluxes, -1), shifted(fluxes, -2)]
    )
    packed = jnp.concatenate(
        [ocean_state.transpose(1, 0, 2), land_mask.astype(jnp.bfloat16)[:, None, :]], axis=1
    )
    packed_low, packed_high = shifted(packed, 1), shifted(packed, -1)
    och = ocean_state.shape[0]
    state_parts = [packed_low[:, :och], packed[:, :och], packed_high[:, :och]]
    mask = jnp.concatenate([packed_low[:, och], packed[:, och], packed_high[:, och]])
    bands = jnp.concatenate([flux_start.astype(jnp.float32)[:, None], flux_weight], axis=1)
    bands = jnp.concatenate([shifted(bands, 1), bands, shifted(bands, -1)])
    flux_matrix = band_matrix(
        bands[:, 0].astype(jnp.int32), bands[:, 1:], position * arows - 2, arows + 4
    )
    ocean_next = ocean_steps(
        state_parts, mask, flux_rows, flux_matrix, conv_first, conv_second, position, band_count
    )
    return (atmos_next, ocean_next.transpose(1, 0, 2))


def solution(mesh):
    in_specs = (
        P(("ens", "lat"), None),
        P(None, ("ens", "lat"), None),
        P("lat", None),
        P(),
        P(),
        P(),
        P(),
        P(),
        P(),
        P(),
        P("lat"),
        P("lat", None),
        P("lat"),
        P("lat", None),
        P(),
        P(),
    )
    out_specs = (P(("ens", "lat"), None), P(None, ("ens", "lat"), None))
    return jax.shard_map(local, mesh=mesh, in_specs=in_specs, out_specs=out_specs, check_vma=False)
```

profile of v0, /device:TPU:9, one launch (start us, length us, event | category | flops | bytes accessed | tf_op | source)
XLA Modules:
  0.0 188.9 jit_solution(3022037490818801576)
XLA Ops:
  0.6 0.8 convert_bitcast_fusion.1
  1.5 0.7 pad_maximum_fusion.3
  2.1 2.6 %collective-permute-start.7 = (f32[4,3]{0,1:T(4,128)S(1)}, f32[4,3]{0,1:T(4,128)S(1)}, u32[]{:S(2)}, u32[]{:S(2)}) collective-permute-start(f32[4,3]{0,1:T(4,128)S(1)} %pad_maximum_fusion.3), channel_id=1, source_target_pairs={{1,0},{2,1},{3,2},{4,3},{5,4},{6,5},{7,6},{8,7},{9,8},{10,9},{11,1... | collective-permute-start | bytes 152 | tf_op jit(solution)/shard_map/ppermute | solution.py:194
  4.7 3.0 %collective-permute-start.6 = (f32[4,3]{0,1:T(4,128)S(1)}, f32[4,3]{0,1:T(4,128)S(1)}, u32[]{:S(2)}, u32[]{:S(2)}) collective-permute-start(f32[4,3]{0,1:T(4,128)S(1)} %pad_maximum_fusion.3), channel_id=1, source_target_pairs={{0,1},{1,2},{2,3},{3,4},{4,5},{5,6},{6,7},{7,8},{8,9},{9,10},{10,1... | collective-permute-start | bytes 152 | tf_op jit(solution)/shard_map/ppermute | solution.py:194
  7.8 0.8 slice_convert_fusion.1
  8.6 2.5 %reshape.231 = f32[4,4,360,4]{3,2,1,0:T(8,128)} reshape(f32[4,4,1440]{2,1,0:T(4,128)S(1)} %slice_convert_fusion.1) | data formatting | bytes 184320 | tf_op jit(solution)/shard_map/reshape | solution.py:43
  11.1 2.8 %reduce_sum.54 = f32[4,4,360]{2,1,0:T(4,128)S(1)} reduce(f32[4,4,360,4]{3,2,1,0:T(8,128)} %reshape.231, f32[]{:T(128)} %constant.78.clone.1), dimensions={3}, to_apply=%region_0.0 | reduce | flops 17280 | bytes 115204 | tf_op jit(solution)/shard_map/reduce_sum | solution.py:42
  14.0 1.9 %collective-permute-start.1 = (bf16[2,1440]{1,0:T(2,128)(2,1)S(1)}, bf16[2,1440]{1,0:T(2,128)(2,1)S(1)}, u32[]{:S(2)}, u32[]{:S(2)}) collective-permute-start(bf16[2,1440]{1,0:T(2,128)(2,1)S(1)} %slice.88), channel_id=1, source_target_pairs={{1,0},{2,1},{3,2},{4,3},{5,4},{6,5},{7,6},{8,7},{9,8},{10,9},{11,1... | collective-permute-start | bytes 17288 | tf_op jit(solution)/shard_map/ppermute | solution.py:22
  16.0 3.6 %collective-permute-start = (bf16[2,1440]{1,0:T(2,128)(2,1)S(1)}, bf16[2,1440]{1,0:T(2,128)(2,1)S(1)}, u32[]{:S(2)}, u32[]{:S(2)}) collective-permute-start(bf16[2,1440]{1,0:T(2,128)(2,1)S(1)} %slice.86), channel_id=1, source_target_pairs={{0,1},{1,2},{2,3},{3,4},{4,5},{5,6},{6,7},{7,8},{8,9},{9,10},{10,1... | collective-permute-start | bytes 17288 | tf_op jit(solution)/shard_map/ppermute | solution.py:19
  19.7 1.6 pad_maximum_fusion.1
  21.3 2.6 %collective-permute-start.8 = (bf16[4,77,1440]{2,0,1:T(4,128)(2,1)}, bf16[4,77,1440]{2,0,1:T(4,128)(2,1)}, u32[]{:S(2)}, u32[]{:S(2)}) collective-permute-start(bf16[4,77,1440]{2,0,1:T(4,128)(2,1)} %pad_maximum_fusion.1), channel_id=1, source_target_pairs={{0,1},{1,2},{2,3},{3,4},{4,5},{5,6},{6,7},{7,8},{8,9},{9,10},{10,1... | collective-permute-start | bytes 2661128 | tf_op jit(solution)/shard_map/ppermute | solution.py:194
  24.0 1.1 copy.60.mid_ref
  25.2 0.1 convert_element_type.77
  25.3 0.7 fusion.63
  26.7 1.2 fusion.7.spread_ref
  28.1 0.3 pad_maximum_fusion.2
  28.5 0.9 copy.62.first_ref
  29.5 0.1 pad.10
  29.6 0.7 copy.81
  30.3 0.6 pad_add_fusion.pos_ref
  31.1 0.1 reshape.221
  31.2 4.5 %fusion.23 = f32[1,4,360]{2,0,1:T(1,128)S(1)} fusion(bf16[4,360,8]{1,0,2:T(4,128)(2,1)S(1)} %reshape.221, f32[]{:T(128)} %bitcast.13, s32[]{:T(128)} %bitcast.12, f32[]{:T(128)} %bitcast.11, s32[]{:T(128)} %bitcast.10, f32[]{:T(128)} %bitcast.9, s32[]{:T(128)} %bitcast.8, f32[]{:T(128)} %bitcast.7, s32[]{:T(128)} %bitcast.6, f32[]{:T(128)} %bitcast.5, ...), kind=kOutput, calls=%fused_computation.45 | convolution fusion | flops 138408 | bytes 28860 | tf_op jit(solution)/shard_map/dot_general | solution.py:229
  35.7 1.6 multiply_reduce_fusion.2
  37.3 5.8 %fusion.12 = f32[360,3072]{1,0:T(8,128)S(1)} fusion(bf16[1024,3072]{1,0:T(8,128)(2,1)} %param.19, f32[360,1024]{1,0:T(8,128)S(1)} %get-tuple-element.25, f32[1024]{0:T(1024)S(1)} %copy-done.15, f32[360]{0:T(512)S(1)} %add_rsqrt_fusion.3), kind=kOutput, calls=%fused_computation.28 | convolution fusion | flops 2266030080 | bytes 12195232 | tf_op jit(solution)/shard_map/dot_general | solution.py:235
  43.1 1.1 slice.122
  44.2 1.9 %collective-permute-start.3 = (bf16[360,1024]{1,0:T(8,128)(2,1)}, bf16[360,1024]{1,0:T(8,128)(2,1)}, u32[]{:S(2)}, u32[]{:S(2)}) collective-permute-start(bf16[360,1024]{1,0:T(8,128)(2,1)} %slice.122), channel_id=1, source_target_pairs={{1,0},{2,1},{3,2},{4,3},{5,4},{6,5},{7,6},{8,7},{9,8},{10,9},{11,1... | collective-permute-start | bytes 2211848 | tf_op jit(solution)/shard_map/ppermute | solution.py:22
  46.1 4.5 %collective-permute-start.2 = (bf16[360,1024]{1,0:T(8,128)(2,1)}, bf16[360,1024]{1,0:T(8,128)(2,1)}, u32[]{:S(2)}, u32[]{:S(2)}) collective-permute-start(bf16[360,1024]{1,0:T(8,128)(2,1)} %slice.122), channel_id=1, source_target_pairs={{0,1},{1,2},{2,3},{3,4},{4,5},{5,6},{6,7},{7,8},{8,9},{9,10},{10,1... | collective-permute-start | bytes 2211848 | tf_op jit(solution)/shard_map/ppermute | solution.py:19
  50.7 1.3 slice_multiply_fusion
  52.0 3.0 %copy.51 = f32[360,1024]{0,1:T(8,128)} copy(f32[360,1024]{1,0:T(8,128)} %slice_multiply_fusion) | data formatting | bytes 2949120 | tf_op jit(solution)/shard_map/mul | solution.py:51
  55.0 1.5 bitcast_reduce_fusion
  56.5 1.3 mul.202
  57.8 3.0 %copy.52 = f32[360,1024]{1,0:T(8,128)} copy(f32[360,1024]{0,1:T(8,128)} %bitcast.100) | data formatting | bytes 2949120 | tf_op jit(solution)/shard_map/mul | solution.py:51
  60.8 4.0 %fusion.61 = (f32[360,1024]{1,0:T(8,128)}, bf16[360,1024]{1,0:T(8,128)(2,1)}) fusion(f32[360,3072]{1,0:T(8,128)} %copy-done.3, f32[360,1024]{1,0:T(8,128)} %copy.52), kind=kLoop, calls=%fused_computation.122 | loop fusion | flops 737280 | bytes 6635520 | tf_op jit(solution)/shard_map/slice | solution.py:237
  64.8 2.4 %collective-permute-start.4 = (bf16[360,1024]{1,0:T(8,128)(2,1)}, bf16[360,1024]{1,0:T(8,128)(2,1)}, u32[]{:S(2)}, u32[]{:S(2)}) collective-permute-start(bf16[360,1024]{1,0:T(8,128)(2,1)} %get-tuple-element.9), channel_id=1, source_target_pairs={{0,1},{1,2},{2,3},{3,4},{4,5},{5,6},{6,7},{7,8},{8,9},{9,10},{10,1... | collective-permute-start | bytes 2211848 | tf_op jit(solution)/shard_map/ppermute | solution.py:19
  67.2 1.9 %collective-permute-start.5 = (bf16[360,1024]{1,0:T(8,128)(2,1)}, bf16[360,1024]{1,0:T(8,128)(2,1)}, u32[]{:S(2)}, u32[]{:S(2)}) collective-permute-start(bf16[360,1024]{1,0:T(8,128)(2,1)} %get-tuple-element.9), channel_id=1, source_target_pairs={{1,0},{2,1},{3,2},{4,3},{5,4},{6,5},{7,6},{8,7},{9,8},{10,9},{11,1... | collective-permute-start | bytes 2211848 | tf_op jit(solution)/shard_map/ppermute | solution.py:22
  69.2 1.5 copy.54
  70.6 3.0 %copy.50 = f32[360,1024]{0,1:T(8,128)} copy(f32[360,1024]{1,0:T(8,128)} %get-tuple-element.8) | data formatting | bytes 2949120 | tf_op jit(solution)/shard_map/slice | solution.py:237
  73.6 1.6 multiply_reduce_fusion
  75.3 4.2 %collective-permute-start.9 = (bf16[4,77,1440]{2,0,1:T(4,128)(2,1)}, bf16[4,77,1440]{2,0,1:T(4,128)(2,1)}, u32[]{:S(2)}, u32[]{:S(2)}) collective-permute-start(bf16[4,77,1440]{2,0,1:T(4,128)(2,1)} %pad_maximum_fusion.1), channel_id=1, source_target_pairs={{1,0},{2,1},{3,2},{4,3},{5,4},{6,5},{7,6},{8,7},{9,8},{10,9},{11,1... | collective-permute-start | bytes 2661128 | tf_op jit(solution)/shard_map/ppermute | solution.py:194
  79.4 3.1 %pad_maximum_fusion = bf16[1080,1024]{1,0:T(8,128)(2,1)} fusion(bf16[360,1024]{1,0:T(8,128)(2,1)} %collective-permute-done.3, bf16[360,1024]{1,0:T(8,128)(2,1)} %slice.122, bf16[360,1024]{1,0:T(8,128)(2,1)} %collective-permute-done.2), kind=kLoop, calls=%fused_computation.8 | loop fusion | flops 6635520 | bytes 4423680 | tf_op jit(solution)/shard_map/concatenate | solution.py:23
  82.6 4.2 %copy.49 = bf16[1080,1024]{0,1:T(8,128)(2,1)} copy(bf16[1080,1024]{1,0:T(8,128)(2,1)} %pad_maximum_fusion) | data formatting | bytes 4423680 | tf_op jit(solution)/shard_map/concatenate | solution.py:23
  86.8 7.2 %collective-permute-done.4 = bf16[360,1024]{1,0:T(8,128)(2,1)} collective-permute-done((bf16[360,1024]{1,0:T(8,128)(2,1)}, bf16[360,1024]{1,0:T(8,128)(2,1)}, u32[]{:S(2)}, u32[]{:S(2)}) %collective-permute-start.4) | collective-permute-done | bytes 737312 | tf_op jit(solution)/shard_map/ppermute | solution.py:19
  94.0 2.3 %copy.53 = bf16[360,1024]{0,1:T(8,128)(2,1)} copy(bf16[360,1024]{1,0:T(8,128)(2,1)} %collective-permute-done.4) | data formatting | bytes 1474560 | tf_op jit(solution)/shard_map/ppermute | solution.py:19
  96.2 2.3 %copy.55 = bf16[360,1024]{0,1:T(8,128)(2,1)} copy(bf16[360,1024]{1,0:T(8,128)(2,1)} %collective-permute-done.5) | data formatting | bytes 1474560 | tf_op jit(solution)/shard_map/ppermute | solution.py:22
  98.5 4.9 %concatenate.39 = bf16[1080,16,64]{0,2,1:T(8,128)(2,1)} concatenate(bf16[360,16,64]{0,2,1:T(8,128)(2,1)} %bitcast.105, bf16[360,16,64]{0,2,1:T(8,128)(2,1)S(1)} %bitcast.104, bf16[360,16,64]{0,2,1:T(8,128)(2,1)} %bitcast.106), dimensions={0} | concatenate | bytes 4423680 | tf_op jit(solution)/shard_map/concatenate | solution.py:23
  103.5 15.0 %fusion.64 = (f32[16,360]{1,0:T(8,128)S(1)}, f32[16,360,1080]{2,1,0:T(8,128)}) fusion(pred[1080]{0:T(1024)(128)(4,1)S(1)} %compare_and_fusion, bf16[1080,16,64]{0,2,1:T(8,128)(2,1)} %concatenate.39, f32[16]{0:T(128)S(1)} %broadcast_multiply_fusion, f32[360,16]{0,1:T(8,128)S(1)} %add_rsqrt_fusion.1, f32[360,1024]{0,1:T(8,128)} %copy.50), kind=kOutput, calls=%fused_computation.125 | convolution fusion | flops 816031808 | bytes 28616824 | tf_op jit(solution)/shard_map/sub | solution.py:60
  118.5 11.5 %fusion.8 = bf16[16,64,360]{2,1,0:T(8,128)(2,1)S(1)} fusion(bf16[1080,16,64]{0,2,1:T(8,128)(2,1)} %bitcast.107, f32[16,360,1080]{2,1,0:T(8,128)} %get-tuple-element.27, f32[16,360]{1,0:T(8,128)S(1)} %get-tuple-element.26), kind=kOutput, calls=%fused_computation.22 | convolution fusion | flops 809072640 | bytes 27855360 | tf_op jit(solution)/shard_map/hqk,khd->qhd/dot_general | solution.py:63
  130.0 1.8 multiply_reduce_fusion.1
  131.9 0.4 fusion.11
  132.3 1.9 %collective-permute-start.10 = (bf16[1,16,360]{2,1,0:T(8,128)(2,1)S(1)}, bf16[1,16,360]{2,1,0:T(8,128)(2,1)S(1)}, u32[]{:S(2)}, u32[]{:S(2)}) collective-permute-start(bf16[1,16,360]{2,1,0:T(8,128)(2,1)S(1)} %fusion.11), channel_id=1, source_target_pairs={{0,2},{1,3},{2,4},{3,5},{4,6},{5,7},{6,8},{7,9},{8,10},{9,11},{10,... | collective-permute-start | bytes 34568 | tf_op jit(solution)/shard_map/ppermute | solution.py:194
  134.2 0.7 select_add_fusion.mat_ref
  134.9 4.4 %collective-permute-start.11 = (bf16[1,16,360]{2,1,0:T(8,128)(2,1)S(1)}, bf16[1,16,360]{2,1,0:T(8,128)(2,1)S(1)}, u32[]{:S(2)}, u32[]{:S(2)}) collective-permute-start(bf16[1,16,360]{2,1,0:T(8,128)(2,1)S(1)} %fusion.11), channel_id=1, source_target_pairs={{0,1},{1,2},{2,3},{3,4},{4,5},{5,6},{6,7},{7,8},{8,9},{9,10},{10,1... | collective-permute-start | bytes 34568 | tf_op jit(solution)/shard_map/ppermute | solution.py:194
  139.3 2.3 %collective-permute-start.12 = (bf16[1,16,360]{2,1,0:T(8,128)(2,1)S(1)}, bf16[1,16,360]{2,1,0:T(8,128)(2,1)S(1)}, u32[]{:S(2)}, u32[]{:S(2)}) collective-permute-start(bf16[1,16,360]{2,1,0:T(8,128)(2,1)S(1)} %fusion.11), channel_id=1, source_target_pairs={{1,0},{2,1},{3,2},{4,3},{5,4},{6,5},{7,6},{8,7},{9,8},{10,9},{11,1... | collective-permute-start | bytes 34568 | tf_op jit(solution)/shard_map/ppermute | solution.py:194
  141.6 4.4 %collective-permute-start.13 = (bf16[1,16,360]{2,1,0:T(8,128)(2,1)S(1)}, bf16[1,16,360]{2,1,0:T(8,128)(2,1)S(1)}, u32[]{:S(2)}, u32[]{:S(2)}) collective-permute-start(bf16[1,16,360]{2,1,0:T(8,128)(2,1)S(1)} %fusion.11), channel_id=1, source_target_pairs={{2,0},{3,1},{4,2},{5,3},{6,4},{7,5},{8,6},{9,7},{10,8},{11,9},{12,... | collective-permute-start | bytes 34568 | tf_op jit(solution)/shard_map/ppermute | solution.py:194
  146.1 0.9 collective-permute-done.13
  147.0 1.5 slice.106
  148.5 1.1 copy.59.low_ref
  149.6 1.5 slice.107
  151.2 1.2 copy.61.high_ref
  152.3 0.7 slice_bitcast_fusion
  153.0 0.7 slice_bitcast_fusion.1
  153.8 0.7 reshape.232.mask_ref
  154.4 31.6 %ocean_steps.1 = bf16[4,76,1440]{2,1,0:T(8,128)(2,1)} custom-call(s32[2]{0:T(128)} %pad_add_fusion.pos_ref, f32[12,5]{1,0:T(8,128)} %select_add_fusion.mat_ref, bf16[4,76,1440]{2,1,0:T(8,128)(2,1)} %copy.59.low_ref, bf16[4,76,1440]{2,1,0:T(8,128)(2,1)} %copy.60.mid_ref, bf16[4,76,1440]{2,1,0:T(8,128)(2,1)} %copy.61.high_ref, ...), custom_call_target="tpu_custom_call" | custom-call | tf_op jit(solution)/shard_map/ocean_steps/pallas_call | solution.py:176
  186.0 2.9 %copy.63 = bf16[76,4,1440]{2,1,0:T(4,128)(2,1)} copy(bf16[76,4,1440]{2,0,1:T(8,128)(2,1)} %bitcast.103) | data formatting | bytes 1751040
  (81 shorter events, 1.0 us)
Async XLA Ops:
  0.6 129.4 %copy-start = (bf16[1024,1024]{1,0:T(8,128)(2,1)S(1)}, bf16[1024,1024]{1,0:T(8,128)(2,1)}, u32[]{:S(2)}) copy-start(bf16[1024,1024]{1,0:T(8,128)(2,1)} %param.20) | copy-start | bytes 6291460
  2.1 28.8 %collective-permute-start.7 = (f32[4,3]{0,1:T(4,128)S(1)}, f32[4,3]{0,1:T(4,128)S(1)}, u32[]{:S(2)}, u32[]{:S(2)}) collective-permute-start(f32[4,3]{0,1:T(4,128)S(1)} %pad_maximum_fusion.3), channel_id=1, source_target_pairs={{1,0},{2,1},{3,2},{4,3},{5,4},{6,5},{7,6},{8,7},{9,8},{10,9},{11,1... | collective-permute-start | bytes 152 | tf_op jit(solution)/shard_map/ppermute | solution.py:194
  4.7 26.2 %collective-permute-start.6 = (f32[4,3]{0,1:T(4,128)S(1)}, f32[4,3]{0,1:T(4,128)S(1)}, u32[]{:S(2)}, u32[]{:S(2)}) collective-permute-start(f32[4,3]{0,1:T(4,128)S(1)} %pad_maximum_fusion.3), channel_id=1, source_target_pairs={{0,1},{1,2},{2,3},{3,4},{4,5},{5,6},{6,7},{7,8},{8,9},{9,10},{10,1... | collective-permute-start | bytes 152 | tf_op jit(solution)/shard_map/ppermute | solution.py:194
  11.1 8.6 %copy-start.8 = (s32[4,1440]{1,0:T(4,128)S(1)}, s32[4,1440]{1,0:T(4,128)}, u32[]{:S(2)}) copy-start(s32[4,1440]{1,0:T(4,128)} %param.18) | copy-start | bytes 69124
  11.1 8.6 %copy-start.4 = (bf16[76,4,1440]{2,1,0:T(4,128)(2,1)S(1)}, bf16[76,4,1440]{2,1,0:T(4,128)(2,1)}, u32[]{:S(2)}) copy-start(bf16[76,4,1440]{2,1,0:T(4,128)(2,1)} %param.17) | copy-start | bytes 2626564
  13.9 11.2 %copy-start.6 = (bf16[9,128,92]{1,2,0:T(8,128)(2,1)S(1)}, bf16[9,128,92]{1,2,0:T(8,128)(2,1)}, u32[]{:S(2)}) copy-start(bf16[9,128,92]{1,2,0:T(8,128)(2,1)} %param.30) | copy-start | bytes 635908
  14.0 17.0 %collective-permute-start.1 = (bf16[2,1440]{1,0:T(2,128)(2,1)S(1)}, bf16[2,1440]{1,0:T(2,128)(2,1)S(1)}, u32[]{:S(2)}, u32[]{:S(2)}) collective-permute-start(bf16[2,1440]{1,0:T(2,128)(2,1)S(1)} %slice.88), channel_id=1, source_target_pairs={{1,0},{2,1},{3,2},{4,3},{5,4},{6,5},{7,6},{8,7},{9,8},{10,9},{11,1... | collective-permute-start | bytes 17288 | tf_op jit(solution)/shard_map/ppermute | solution.py:22
  16.0 15.0 %collective-permute-start = (bf16[2,1440]{1,0:T(2,128)(2,1)S(1)}, bf16[2,1440]{1,0:T(2,128)(2,1)S(1)}, u32[]{:S(2)}, u32[]{:S(2)}) collective-permute-start(bf16[2,1440]{1,0:T(2,128)(2,1)S(1)} %slice.86), channel_id=1, source_target_pairs={{0,1},{1,2},{2,3},{3,4},{4,5},{5,6},{6,7},{7,8},{8,9},{9,10},{10,1... | collective-permute-start | bytes 17288 | tf_op jit(solution)/shard_map/ppermute | solution.py:19
  19.7 5.5 %copy-start.11 = (f32[1,7]{1,0:T(1,128)S(1)}, f32[1,7]{1,0:T(1,128)}, u32[]{:S(2)}) copy-start(f32[1,7]{1,0:T(1,128)} %param.29) | copy-start | bytes 88
  19.7 6.9 %copy-start.16 = (f32[16]{0:T(128)S(1)}, f32[16]{0:T(128)}, u32[]{:S(2)}) copy-start(f32[16]{0:T(128)} %param.21) | copy-start | bytes 196
  21.3 125.7 %collective-permute-start.8 = (bf16[4,77,1440]{2,0,1:T(4,128)(2,1)}, bf16[4,77,1440]{2,0,1:T(4,128)(2,1)}, u32[]{:S(2)}, u32[]{:S(2)}) collective-permute-start(bf16[4,77,1440]{2,0,1:T(4,128)(2,1)} %pad_maximum_fusion.1), channel_id=1, source_target_pairs={{0,1},{1,2},{2,3},{3,4},{4,5},{5,6},{6,7},{7,8},{8,9},{9,10},{10,1... | collective-permute-start | bytes 2661128 | tf_op jit(solution)/shard_map/ppermute | solution.py:194
  25.1 4.3 %copy-start.7 = (bf16[9,76,128]{2,1,0:T(8,128)(2,1)S(1)}, bf16[9,76,128]{2,1,0:T(8,128)(2,1)}, u32[]{:S(2)}) copy-start(bf16[9,76,128]{2,1,0:T(8,128)(2,1)} %param.31) | copy-start | bytes 525316
  26.6 4.3 %copy-start.14 = (f32[4,2]{0,1:T(2,128)S(1)}, f32[4,2]{0,1:T(2,128)}, u32[]{:S(2)}) copy-start(f32[4,2]{0,1:T(2,128)} %param.27) | copy-start | bytes 100
  27.9 7.7 %copy-start.5 = (bf16[360,1024]{1,0:T(8,128)(2,1)S(1)}, bf16[360,1024]{1,0:T(8,128)(2,1)}, u32[]{:S(2)}) copy-start(bf16[360,1024]{1,0:T(8,128)(2,1)} %param.16) | copy-start | bytes 2211844
  27.9 7.7 %copy-start.12 = (f32[4,1024]{1,0:T(4,128)S(1)}, f32[4,1024]{1,0:T(4,128)}, u32[]{:S(2)}) copy-start(f32[4,1024]{1,0:T(4,128)} %param.25) | copy-start | bytes 49156
  28.5 8.7 %copy-start.15 = (f32[1024]{0:T(1024)S(1)}, f32[1024]{0:T(1024)}, u32[]{:S(2)}) copy-start(f32[1024]{0:T(1024)} %param.22) | copy-start | bytes 12292
  37.2 5.9 %copy-start.1 = (f32[360,1024]{1,0:T(8,128)}, f32[360,1024]{1,0:T(8,128)S(1)}, u32[]{:S(2)}) copy-start(f32[360,1024]{1,0:T(8,128)S(1)} %get-tuple-element.25) | copy-start | bytes 4423684
  43.1 7.6 %copy-start.3 = (f32[360,3072]{1,0:T(8,128)}, f32[360,3072]{1,0:T(8,128)S(1)}, u32[]{:S(2)}) copy-start(f32[360,3072]{1,0:T(8,128)S(1)} %fusion.12) | copy-start | bytes 13271044
  44.2 31.0 %collective-permute-start.3 = (bf16[360,1024]{1,0:T(8,128)(2,1)}, bf16[360,1024]{1,0:T(8,128)(2,1)}, u32[]{:S(2)}, u32[]{:S(2)}) collective-permute-start(bf16[360,1024]{1,0:T(8,128)(2,1)} %slice.122), channel_id=1, source_target_pairs={{1,0},{2,1},{3,2},{4,3},{5,4},{6,5},{7,6},{8,7},{9,8},{10,9},{11,1... | collective-permute-start | bytes 2211848 | tf_op jit(solution)/shard_map/ppermute | solution.py:22
  46.1 33.3 %collective-permute-start.2 = (bf16[360,1024]{1,0:T(8,128)(2,1)}, bf16[360,1024]{1,0:T(8,128)(2,1)}, u32[]{:S(2)}, u32[]{:S(2)}) collective-permute-start(bf16[360,1024]{1,0:T(8,128)(2,1)} %slice.122), channel_id=1, source_target_pairs={{0,1},{1,2},{2,3},{3,4},{4,5},{5,6},{6,7},{7,8},{8,9},{9,10},{10,1... | collective-permute-start | bytes 2211848 | tf_op jit(solution)/shard_map/ppermute | solution.py:19
  64.8 29.1 %collective-permute-start.4 = (bf16[360,1024]{1,0:T(8,128)(2,1)}, bf16[360,1024]{1,0:T(8,128)(2,1)}, u32[]{:S(2)}, u32[]{:S(2)}) collective-permute-start(bf16[360,1024]{1,0:T(8,128)(2,1)} %get-tuple-element.9), channel_id=1, source_target_pairs={{0,1},{1,2},{2,3},{3,4},{4,5},{5,6},{6,7},{7,8},{8,9},{9,10},{10,1... | collective-permute-start | bytes 2211848 | tf_op jit(solution)/shard_map/ppermute | solution.py:19
  67.2 29.0 %collective-permute-start.5 = (bf16[360,1024]{1,0:T(8,128)(2,1)}, bf16[360,1024]{1,0:T(8,128)(2,1)}, u32[]{:S(2)}, u32[]{:S(2)}) collective-permute-start(bf16[360,1024]{1,0:T(8,128)(2,1)} %get-tuple-element.9), channel_id=1, source_target_pairs={{1,0},{2,1},{3,2},{4,3},{5,4},{6,5},{7,6},{8,7},{9,8},{10,9},{11,1... | collective-permute-start | bytes 2211848 | tf_op jit(solution)/shard_map/ppermute | solution.py:22
  75.3 74.4 %collective-permute-start.9 = (bf16[4,77,1440]{2,0,1:T(4,128)(2,1)}, bf16[4,77,1440]{2,0,1:T(4,128)(2,1)}, u32[]{:S(2)}, u32[]{:S(2)}) collective-permute-start(bf16[4,77,1440]{2,0,1:T(4,128)(2,1)} %pad_maximum_fusion.1), channel_id=1, source_target_pairs={{1,0},{2,1},{3,2},{4,3},{5,4},{6,5},{7,6},{8,7},{9,8},{10,9},{11,1... | collective-permute-start | bytes 2661128 | tf_op jit(solution)/shard_map/ppermute | solution.py:194
  118.5 11.5 %copy-start.2 = (f32[360,1024]{1,0:T(8,128)S(1)}, f32[360,1024]{1,0:T(8,128)}, u32[]{:S(2)}) copy-start(f32[360,1024]{1,0:T(8,128)} %copy-done.1) | copy-start | bytes 4423684
  130.0 1.9 copy-start.10
  130.0 1.9 copy-start.13
  132.3 9.3 %collective-permute-start.10 = (bf16[1,16,360]{2,1,0:T(8,128)(2,1)S(1)}, bf16[1,16,360]{2,1,0:T(8,128)(2,1)S(1)}, u32[]{:S(2)}, u32[]{:S(2)}) collective-permute-start(bf16[1,16,360]{2,1,0:T(8,128)(2,1)S(1)} %fusion.11), channel_id=1, source_target_pairs={{0,2},{1,3},{2,4},{3,5},{4,6},{5,7},{6,8},{7,9},{8,10},{9,11},{10,... | collective-permute-start | bytes 34568 | tf_op jit(solution)/shard_map/ppermute | solution.py:194
  134.9 11.1 %collective-permute-start.11 = (bf16[1,16,360]{2,1,0:T(8,128)(2,1)S(1)}, bf16[1,16,360]{2,1,0:T(8,128)(2,1)S(1)}, u32[]{:S(2)}, u32[]{:S(2)}) collective-permute-start(bf16[1,16,360]{2,1,0:T(8,128)(2,1)S(1)} %fusion.11), channel_id=1, source_target_pairs={{0,1},{1,2},{2,3},{3,4},{4,5},{5,6},{6,7},{7,8},{8,9},{9,10},{10,1... | collective-permute-start | bytes 34568 | tf_op jit(solution)/shard_map/ppermute | solution.py:194
  139.3 6.8 %collective-permute-start.12 = (bf16[1,16,360]{2,1,0:T(8,128)(2,1)S(1)}, bf16[1,16,360]{2,1,0:T(8,128)(2,1)S(1)}, u32[]{:S(2)}, u32[]{:S(2)}) collective-permute-start(bf16[1,16,360]{2,1,0:T(8,128)(2,1)S(1)} %fusion.11), channel_id=1, source_target_pairs={{1,0},{2,1},{3,2},{4,3},{5,4},{6,5},{7,6},{8,7},{9,8},{10,9},{11,1... | collective-permute-start | bytes 34568 | tf_op jit(solution)/shard_map/ppermute | solution.py:194
  141.6 5.4 %collective-permute-start.13 = (bf16[1,16,360]{2,1,0:T(8,128)(2,1)S(1)}, bf16[1,16,360]{2,1,0:T(8,128)(2,1)S(1)}, u32[]{:S(2)}, u32[]{:S(2)}) collective-permute-start(bf16[1,16,360]{2,1,0:T(8,128)(2,1)S(1)} %fusion.11), channel_id=1, source_target_pairs={{2,0},{3,1},{4,2},{5,3},{6,4},{7,5},{8,6},{9,7},{10,8},{11,9},{12,... | collective-permute-start | bytes 34568 | tf_op jit(solution)/shard_map/ppermute | solution.py:194
  147.0 4.2 %copy-start.9 = (bf16[5,16,360]{2,1,0:T(8,128)(2,1)}, bf16[5,16,360]{2,1,0:T(8,128)(2,1)S(1)}, u32[]{:S(2)}) copy-start(bf16[5,16,360]{2,1,0:T(8,128)(2,1)S(1)} %constant_dynamic-update-slice_fusion.flux_ref) | copy-start | bytes 172804
where the time goes:
time: 192 us; the launch traced here: 189 us
  local copies, waits for them, and re-layouts  43.6 us (23%)
  starting transfers between devices  41.7 us (22%)
  matrix products  40.7 us (21%)
  Pallas kernels  31.6 us (16%)
  other arithmetic  21.3 us (11%)
  waiting for transfers between devices  8.13 us (4%)
    pallas_call x1, Pallas kernels, ocean_steps(): pl.pallas_call(ocean_kernel, out_shape=jax.ShapeDtypeStruct((orows, och,...  31.6 us
    ppermute x8, starting transfers between devices, shifted(): return lax.ppermute(block, 'lat', pairs)  25.4 us
    sub x1, matrix products, attend(): raised = jnp.exp(scores - largest)  15 us
    dot_general x1, matrix products, attend(): jnp.einsum('hqk,khd->qhd', probs, value_heads, preferred_element_type=jnp...  11.5 us
    ppermute x3, starting transfers between devices, padded_2(): lax.ppermute(lax.slice_in_dim(block, block.shape[dim] - width, None, axis...  10.6 us
    concatenate x2, local copies, waits for them, and re-layouts, padded_2(): block = jnp.concatenate([low, block, high], axis=dim)  9.15 us
    ppermute x3, waiting for transfers between devices, padded_2(): lax.ppermute(lax.slice_in_dim(block, block.shape[dim] - width, None, axis...  7.21 us
    dot_general x1, matrix products, local(): qkv = jnp.dot(normed, w_qkv, preferred_element_type=jnp.float32)  5.85 us
  transfers between devices with their start and end apart: 14, of which 2 were waited for; matrix products, arithmetic and copies ran while one was open for 51% of the time, Pallas kernels for 0%

commit v1 on v0

v1 whole, which is shorter than its diff:
```python
import jax
import jax.numpy as jnp
from jax import lax
from jax.experimental import pallas as pl
from jax.experimental.pallas import tpu as pltpu
from jax.sharding import PartitionSpec as P

LEVELS = 19
VARS = 4
SPAN = 4
OSTEPS = 2


def rms_norm(values, scaling):
    return values * lax.rsqrt(jnp.mean(values * values, axis=-1, keepdims=True) + 1e-06) * scaling


def band_matrix(starts, weight, first_col, col_count):
    columns = first_col + jnp.arange(col_count, dtype=jnp.int32)
    summed = jnp.zeros((starts.shape[0], col_count), jnp.float32)
    for offset in range(weight.shape[1]):
        matches = (columns[None, :] == starts[:, None] + offset).astype(jnp.float32)
        summed = summed + weight[:, offset : offset + 1] * matches
    return summed


def atmos_kernel(surf_mat, flux_mat, scale_ref, atmos_ref, top_ref, mean_ref, embed_ref, gain_ref,
                 flux_gain_ref, qkv_ref, wout_ref, wflux_ref, ocean_ref,
                 after_ref, flux_mid, flux_low, flux_high, ocean_low, ocean_high,
                 surf, near, near_q, near_k, near_v, held, rows, send_sems, recv_sems):
    me = lax.axis_index("lat")
    count = lax.axis_size("lat")
    token_count, width = atmos_ref.shape
    group = near_q.shape[2]
    groups = width // group
    depth = width // scale_ref.shape[0]
    per_group = group // depth
    has = (me > 0, me < count - 1)
    target = (me - 1, me + 1)

    def send(kind, side, source, dest):
        return pltpu.make_async_remote_copy(
            src_ref=source,
            dst_ref=dest,
            send_sem=send_sems.at[kind, side],
            recv_sem=recv_sems.at[kind, side],
            device_id={"lat": target[side]},
            device_id_type=pl.DeviceIdType.MESH,
        )

    def start_both(kind, source, to_high, to_low):
        @pl.when(has[0])
        def _():
            send(kind, 0, source, to_high).start()

        @pl.when(has[1])
        def _():
            send(kind, 1, source, to_low).start()

    def wait_both(kind, source, to_high, to_low):
        @pl.when(has[0])
        def _():
            send(kind, 1, source, to_low).wait_recv()
            send(kind, 0, source, to_high).wait_send()

        @pl.when(has[1])
        def _():
            send(kind, 0, source, to_high).wait_recv()
            send(kind, 1, source, to_low).wait_send()

    barrier = pltpu.get_barrier_semaphore()
    for side in range(2):
        @pl.when(has[side])
        def _(side=side):
            pl.semaphore_signal(
                barrier, inc=1, device_id={"lat": target[side]},
                device_id_type=pl.DeviceIdType.MESH,
            )

    @pl.when(jnp.logical_not(has[0]))
    def _():
        surf[0] = jnp.zeros_like(surf[0])
        near[0] = jnp.zeros_like(near[0])
        rows[0] = jnp.zeros_like(rows[0])
        flux_low[...] = jnp.zeros_like(flux_low)

    @pl.when(jnp.logical_not(has[1]))
    def _():
        surf[2] = jnp.zeros_like(surf[2])
        near[2] = jnp.zeros_like(near[2])
        rows[2] = jnp.zeros_like(rows[2])
        flux_high[...] = jnp.zeros_like(flux_high)

    surf[1] = (
        jnp.dot(top_ref[...], mean_ref[...], preferred_element_type=jnp.float32) * (1.0 / SPAN)
    ).astype(jnp.bfloat16)
    pl.semaphore_wait(barrier, jnp.where(has[0], 1, 0) + jnp.where(has[1], 1, 0))
    surf_args = (0, surf.at[1], surf.at[2], surf.at[0])
    start_both(*surf_args)
    wait_both(*surf_args)
    band = jnp.zeros((VARS, surf.shape[2]), jnp.float32)
    for part in range(3):
        block = surf[part].astype(jnp.float32)
        for i in range(block.shape[0] // VARS):
            weight = surf_mat[0, part * (block.shape[0] // VARS) + i]
            band = band + weight * block[i * VARS : (i + 1) * VARS]
    band = jnp.concatenate([band, jnp.zeros_like(band)], axis=0)
    started = atmos_ref[...].astype(jnp.float32) + lax.dot_general(
        band, embed_ref[...], (((0,), (0,)), ((), ())), precision=lax.Precision.HIGHEST,
        preferred_element_type=jnp.float32,
    )
    held[...] = started
    near[1] = rms_norm(started, gain_ref[...]).astype(jnp.bfloat16)
    near_args = (1, near.at[1], near.at[2], near.at[0])
    ocean_args = (2, ocean_ref, ocean_high, ocean_low)
    start_both(*near_args)
    start_both(*ocean_args)

    lane = lax.broadcasted_iota(jnp.int32, (1, group), 1) // depth

    def head_scales(raw):
        squares = raw * raw
        factor = jnp.zeros_like(raw)
        for h in range(per_group):
            total = jnp.sum(jnp.where(lane == h, squares, 0.0), axis=1, keepdims=True)
            factor = jnp.where(lane == h, lax.rsqrt(total * (1.0 / depth) + 1e-06), factor)
        return raw * factor

    def project(part, column):
        return jnp.dot(
            near[part], qkv_ref[:, pl.ds(pl.multiple_of(column, group), group)],
            preferred_element_type=jnp.float32,
        )

    def own(g, carry):
        column = g * group
        query = head_scales(project(1, column))
        scale = jnp.zeros((1, group), jnp.float32)
        for h in range(per_group):
            scale = jnp.where(lane == h, scale_ref[g * per_group + h], scale)
        near_q[g] = (query * (scale * (1.0 / depth**0.5))).astype(jnp.bfloat16)
        near_k[g, 1] = head_scales(project(1, width + column)).astype(jnp.bfloat16)
        near_v[g, 1] = project(1, 2 * width + column).astype(jnp.bfloat16)
        return carry

    lax.fori_loop(0, groups, own, 0)
    wait_both(*near_args)

    def attend(g, carry):
        column = g * group
        for part in (0, 2):
            near_k[g, part] = head_scales(project(part, width + column)).astype(jnp.bfloat16)
            near_v[g, part] = project(part, 2 * width + column).astype(jnp.bfloat16)
        queries = near_q[g]
        mixed = jnp.zeros((token_count, group), jnp.float32)
        for h in range(per_group):
            query = jnp.where(lane == h, queries, jnp.zeros_like(queries))
            scores = []
            for part in range(3):
                score = lax.dot_general(
                    query, near_k[g, part], (((1,), (1,)), ((), ())),
                    preferred_element_type=jnp.float32,
                )
                if part != 1:
                    score = jnp.where(has[part // 2], score, -1e30)
                scores.append(score)
            largest = jnp.max(jnp.maximum(jnp.maximum(scores[0], scores[1]), scores[2]),
                              axis=1, keepdims=True)
            raised = [jnp.exp(score - largest) for score in scores]
            total = jnp.sum(raised[0] + raised[1] + raised[2], axis=1, keepdims=True)
            inverse = 1.0 / total
            value = jnp.zeros((token_count, group), jnp.float32)
            for part in range(3):
                value = value + jnp.dot(
                    (raised[part] * inverse).astype(jnp.bfloat16), near_v[g, part],
                    preferred_element_type=jnp.float32,
                )
            mixed = jnp.where(lane == h, value, mixed)
        held[...] += jnp.dot(
            mixed.astype(jnp.bfloat16), wout_ref[pl.ds(pl.multiple_of(column, group), group), :],
            preferred_element_type=jnp.float32,
        )
        return carry

    lax.fori_loop(0, groups, attend, 0)
    after = held[...]
    after_ref[...] = after.astype(jnp.bfloat16)
    flux_in = rms_norm(after, flux_gain_ref[...]).astype(jnp.bfloat16)
    rows[1] = lax.dot_general(
        wflux_ref[...], flux_in, (((1,), (1,)), ((), ())), preferred_element_type=jnp.float32
    ).astype(jnp.bfloat16)
    rows_args = (3, rows.at[1], rows.at[2], rows.at[0])
    start_both(*rows_args)
    wait_both(*rows_args)
    sources = [rows[part].astype(jnp.float32) for part in range(3)]
    for i in range(flux_mid.shape[0]):
        flux_mid[i] = (
            flux_mat[i, 0] * sources[0] + flux_mat[i, 1] * sources[1] + flux_mat[i, 2] * sources[2]
        ).astype(jnp.bfloat16)
    flux_args = (4, flux_mid, flux_high, flux_low)
    start_both(*flux_args)
    wait_both(*ocean_args)
    wait_both(*flux_args)


def atmos_block(surf_mat, flux_mat, head_scale, atmos, top, gain_attn, gain_flux, w_qkv, w_out,
                w_flux, surf_embed, packed):
    token_count, width = atmos.shape
    alon = top.shape[1] // SPAN
    orows = packed.shape[0]
    nflux = w_flux.shape[1]
    group = 256
    groups = width // group
    index = jnp.arange(top.shape[1], dtype=jnp.int32) // SPAN
    mean = (index[:, None] == jnp.arange(alon, dtype=jnp.int32)[None, :]).astype(jnp.bfloat16)
    embed = jnp.pad(surf_embed, ((0, VARS), (0, 0)))
    vmem = pl.BlockSpec(memory_space=pltpu.VMEM)
    smem = pl.BlockSpec(memory_space=pltpu.SMEM)
    anywhere = pl.BlockSpec(memory_space=pl.ANY)
    flux_shape = jax.ShapeDtypeStruct((orows, nflux, alon), jnp.bfloat16)
    ocean_shape = jax.ShapeDtypeStruct(packed.shape, packed.dtype)
    return pl.pallas_call(
        atmos_kernel,
        out_shape=[
            jax.ShapeDtypeStruct((token_count, width), jnp.bfloat16),
            flux_shape, flux_shape, flux_shape, ocean_shape, ocean_shape,
        ],
        in_specs=[smem] * 3 + [vmem] * 9 + [anywhere],
        out_specs=[vmem] * 4 + [anywhere] * 2,
        scratch_shapes=[
            pltpu.VMEM((3, top.shape[0], alon), jnp.bfloat16),
            pltpu.VMEM((3, token_count, width), jnp.bfloat16),
            pltpu.VMEM((groups, token_count, group), jnp.bfloat16),
            pltpu.VMEM((groups, 3, token_count, group), jnp.bfloat16),
            pltpu.VMEM((groups, 3, token_count, group), jnp.bfloat16),
            pltpu.VMEM((token_count, width), jnp.float32),
            pltpu.VMEM((3, nflux, alon), jnp.bfloat16),
            pltpu.SemaphoreType.DMA((5, 2)),
            pltpu.SemaphoreType.DMA((5, 2)),
        ],
        compiler_params=pltpu.CompilerParams(
            collective_id=0, has_side_effects=True, vmem_limit_bytes=58 * 1024 * 1024
        ),
        name="atmos_block",
    )(surf_mat, flux_mat, head_scale, atmos, top, mean, embed, gain_attn[None, :],
      gain_flux[None, :], w_qkv, w_out, w_flux.T, packed)


def ocean_kernel(pos_ref, low_ref, mid_ref, high_ref,
                 flux_low, flux_mid, flux_high, spread_ref,
                 first_ref, second_ref, out_ref, xs, hs, st, sea):
    och = mid_ref.shape[1] - 1
    olon = mid_ref.shape[2]
    orows = mid_ref.shape[0]
    wide = xs.shape[1]
    nflux = flux_mid.shape[1]
    hid = first_ref.shape[0] // 3
    opad = second_ref.shape[0] // 3
    stride = opad + nflux
    first_row = pos_ref[0]
    total = pos_ref[1]
    tail = wide - 128
    first_pad = olon - tail

    def wrap(head, last):
        lane = lax.broadcasted_iota(jnp.int32, last.shape, 1)
        end = pltpu.roll(last, 128 - first_pad, 1)
        begin = pltpu.roll(head, first_pad, 1)
        return jnp.where(lane == first_pad, begin, jnp.where(lane == 127, end, last))

    def combine(full, size):
        left = pltpu.roll(full[0:size], 1, 1)
        right = pltpu.roll(full[2 * size : 3 * size], wide - 1, 1)
        return left + full[size : 2 * size] + right

    sides = ((low_ref, flux_low), (mid_ref, flux_mid), (high_ref, flux_high))
    for part, (ref, flux) in enumerate(sides):
        def fill(i, carry, ref=ref, flux=flux, part=part):
            row = part * orows + i
            place = first_row + row - orows
            packed = ref[i].astype(jnp.float32)
            packed = jnp.where((place >= 0) & (place < total), packed, 0.0)
            state = packed[0:och]
            sea[row, :, 0:tail] = packed[och:, 0:tail]
            sea[row, :, tail:] = jnp.concatenate(
                [packed[och:, tail:], jnp.zeros((1, wide - olon), jnp.float32)], axis=1
            )
            state = jnp.concatenate([state, jnp.zeros((opad - och, olon), jnp.float32)], axis=0)
            last = jnp.concatenate(
                [state[:, tail:], jnp.zeros((opad, wide - olon), jnp.float32)], axis=1
            )
            st[row, :, 0:tail] = state[:, 0:tail]
            st[row, :, tail:] = wrap(state[:, 0:128], last)
            base = pl.multiple_of(row * stride, 16)
            xs[pl.ds(base, opad), :] = st[row].astype(jnp.bfloat16)
            spread = jnp.dot(flux[i], spread_ref[...], preferred_element_type=jnp.float32)
            base = pl.multiple_of(row * stride + opad, 16)
            xs[pl.ds(base, nflux), :] = spread.astype(jnp.bfloat16)
            return carry
        lax.fori_loop(0, orows, fill, 0)

    for step in range(OSTEPS):
        edge = 1 + 2 * step

        def first(row, carry):
            block = xs[pl.ds(pl.multiple_of((row - 1) * stride, 16), 3 * stride), :]
            full = jnp.dot(first_ref[...], block, preferred_element_type=jnp.float32)
            hidden = jax.nn.gelu(combine(full, hid), approximate=True)
            place = first_row + row - orows
            inside = jnp.where((place >= 0) & (place < total), 1.0, 0.0).astype(jnp.float32)
            hidden = hidden * inside
            base = pl.multiple_of(row * hid, 16)
            hs[pl.ds(base, hid), 0:tail] = hidden[:, 0:tail].astype(jnp.bfloat16)
            hs[pl.ds(base, hid), tail:] = wrap(hidden[:, 0:128], hidden[:, tail:]).astype(jnp.bfloat16)
            return carry
        lax.fori_loop(edge, 3 * orows - edge, first, 0)

        def second(row, carry):
            block = hs[pl.ds(pl.multiple_of((row - 1) * hid, 16), 3 * hid), :]
            full = jnp.dot(second_ref[...], block, preferred_element_type=jnp.float32)
            state = st[row] + sea[row] * combine(full, opad)
            if step == OSTEPS - 1:
                out_ref[row - orows] = state[0:och, 0:olon].astype(jnp.bfloat16)
            else:
                st[row, :, 0:tail] = state[:, 0:tail]
                st[row, :, tail:] = wrap(state[:, 0:128], state[:, tail:])
                base = pl.multiple_of(row * stride, 16)
                xs[pl.ds(base, opad), :] = st[row].astype(jnp.bfloat16)
            return carry
        lax.fori_loop(edge + 1, 3 * orows - edge - 1, second, 0)


def round_up(value, unit):
    return (value + unit - 1) // unit * unit


def ocean_steps(state_parts, fluxes, conv_first, conv_second, position, band_count):
    orows, _, olon = state_parts[1].shape
    och = conv_second.shape[1]
    nflux = fluxes[1].shape[1]
    hid = conv_first.shape[1]
    opad = round_up(och, 16)
    wide = round_up(olon + 2, 128)
    alon = fluxes[1].shape[2]
    first = conv_first.reshape(3, 3, hid, och + nflux)
    first = jnp.concatenate(
        [first[..., :och], jnp.zeros((3, 3, hid, opad - och), first.dtype), first[..., och:]], axis=3
    )
    first = first.transpose(1, 2, 0, 3).reshape(3 * hid, 3 * (opad + nflux))
    second = jnp.pad(conv_second.reshape(3, 3, och, hid), ((0, 0), (0, 0), (0, opad - och), (0, 0)))
    second = second.transpose(1, 2, 0, 3).reshape(3 * opad, 3 * hid)
    column = jnp.arange(wide, dtype=jnp.int32)
    longitude = jnp.where(column < olon, column, jnp.where(column == olon, 0, olon - 1))
    spread = (longitude[None, :] // SPAN == jnp.arange(alon, dtype=jnp.int32)[:, None]).astype(jnp.bfloat16)
    scalars = jnp.stack([position * orows, band_count * orows]).astype(jnp.int32)
    vmem = pl.BlockSpec(memory_space=pltpu.VMEM)
    smem = pl.BlockSpec(memory_space=pltpu.SMEM)
    return pl.pallas_call(
        ocean_kernel,
        out_shape=jax.ShapeDtypeStruct((orows, och, olon), jnp.bfloat16),
        in_specs=[smem] + [vmem] * 9,
        out_specs=vmem,
        scratch_shapes=[
            pltpu.VMEM((3 * orows * (opad + nflux), wide), jnp.bfloat16),
            pltpu.VMEM((3 * orows * hid, wide), jnp.bfloat16),
            pltpu.VMEM((3 * orows, opad, wide), jnp.float32),
            pltpu.VMEM((3 * orows, 1, wide), jnp.float32),
        ],
        compiler_params=pltpu.CompilerParams(vmem_limit_bytes=60 * 1024 * 1024),
        name="ocean_steps",
    )(scalars, *state_parts, *fluxes, spread, first, second)


def local(
    atmos,
    ocean_state,
    land_mask,
    w_qkv,
    w_out,
    head_scale,
    gain_attn,
    gain_flux,
    w_flux,
    surf_embed,
    flux_start,
    flux_weight,
    surf_start,
    surf_weight,
    conv_first,
    conv_second,
):
    position = lax.axis_index("lat")
    band_count = lax.axis_size("lat")
    orows = ocean_state.shape[1]
    packed = jnp.concatenate(
        [ocean_state.transpose(1, 0, 2), land_mask.astype(jnp.bfloat16)[:, None, :]], axis=1
    )
    top = ocean_state[::LEVELS].transpose(1, 0, 2).reshape(orows * VARS, -1)
    first_column = (position - 1) * orows
    surf_mat = band_matrix(surf_start, surf_weight, first_column, 3 * orows)
    columns = first_column + jnp.arange(3 * orows, dtype=jnp.int32)
    surf_mat = jnp.where((columns >= 0) & (columns < band_count * orows), surf_mat, 0.0)
    flux_mat = band_matrix(flux_start, flux_weight, position - 1, 3)
    atmos_next, flux_mid, flux_low, flux_high, ocean_low, ocean_high = atmos_block(
        surf_mat, flux_mat, head_scale, atmos, top, gain_attn, gain_flux, w_qkv, w_out, w_flux,
        surf_embed, packed,
    )
    ocean_next = ocean_steps(
        [ocean_low, packed, ocean_high], [flux_low, flux_mid, flux_high], conv_first, conv_second,
        position, band_count,
    )
    return (atmos_next, ocean_next.transpose(1, 0, 2))


def solution(mesh):
    in_specs = (
        P(("ens", "lat"), None),
        P(None, ("ens", "lat"), None),
        P("lat", None),
        P(),
        P(),
        P(),
        P(),
        P(),
        P(),
        P(),
        P("lat"),
        P("lat", None),
        P("lat"),
        P("lat", None),
        P(),
        P(),
    )
    out_specs = (P(("ens", "lat"), None), P(None, ("ens", "lat"), None))
    return jax.shard_map(local, mesh=mesh, in_specs=in_specs, out_specs=out_specs, check_vma=False)
```

time: 192 us -> 120 us (0.62); the launches traced: 189 us -> 120 us
  Pallas kernels: 31.6 us -> 94.9 us
  starting transfers between devices: 41.7 us -> 0 us
  matrix products: 40.7 us -> 0 us
  local copies, waits for them, and re-layouts: 43.6 us -> 11.2 us
  other arithmetic: 21.3 us -> 12.3 us
  waiting for transfers between devices: 8.13 us -> 0 us
    pallas_call x0 -> x1, Pallas kernels: none -> 64.6 us  [atmos_block(): pl.pallas_call(atmos_kernel, out_shape=[jax.ShapeDtypeStruct((token_count...]
    ppermute x14 -> x0, starting transfers between devices: 41.7 us -> none  [the longest x8 25.4 us: shifted(): return lax.ppermute(block, 'lat', pairs)]
    dot_general x6 -> x0, matrix products: 25.7 us -> none  [the longest x1 11.5 us: attend(): jnp.einsum('hqk,khd->qhd', probs, value_heads, preferred_element_type=jnp...]
    sub x1 -> x0, matrix products: 15 us -> none  [attend(): raised = jnp.exp(scores - largest)]
    slice x11 -> x0, local copies, waits for them, and re-layouts: 9.58 us -> none  [the longest x4 5.3 us: local(): state_parts = [packed_low[:, :och], packed[:, :och], packed_high[:, :och]]]
    concatenate x3 -> x0, local copies, waits for them, and re-layouts: 9.15 us -> none  [the longest x2 9.15 us: padded_2(): block = jnp.concatenate([low, block, high], axis=dim)]
    ppermute x14 -> x0, waiting for transfers between devices: 8.13 us -> none  [the longest x3 7.21 us: padded_2(): lax.ppermute(lax.slice_in_dim(block, block.shape[dim] - width, None, axis...]
    mul x3 -> x1, local copies, waits for them, and re-layouts: 7.28 us -> 0.76 us  [band_matrix(): summed = summed + weight[:, offset:offset + 1] * matches]
  transfers between devices with their start and end apart: 14 -> 0, of which waited for: 2 -> 0; matrix products, arithmetic and copies ran while one was open for 51% -> 0% of each run, Pallas kernels for 0% -> 0%
where the time goes in v1:
time: 120 us
  Pallas kernels  94.9 us (79%)
  other arithmetic  12.3 us (10%)
  local copies, waits for them, and re-layouts  11.2 us (9%)
  between operations  1.42 us (1%)
    pallas_call x1, Pallas kernels, atmos_block(): pl.pallas_call(atmos_kernel, out_shape=[jax.ShapeDtypeStruct((token_count...  64.6 us
    pallas_call x1, Pallas kernels, ocean_steps(): pl.pallas_call(ocean_kernel, out_shape=jax.ShapeDtypeStruct((orows, och,...  30.3 us
    select_n x1, other arithmetic, local(): jnp.where((columns >= 0) & (columns < band_count * orows), surf_mat, 0.0)  5.01 us
    unnamed x15, local copies, waits for them, and re-layouts  4.81 us

profile of v1, /device:TPU:9, one launch (start us, length us, event | category | flops | bytes accessed | tf_op | source)
XLA Modules:
  0.0 119.8 jit_solution(17064517815667977192)
XLA Ops:
  0.6 0.0 copy-start
  0.6 1.6 %fusion.12 = (f32[1,1]{1,0:T(1,128)}, f32[1,1]{1,0:T(1,128)}, f32[1,1]{1,0:T(1,128)}, f32[1,1]{1,0:T(1,128)}, f32[1,1]{1,0:T(1,128)}, /*index=5*/f32[1,1]{1,0:T(1,128)}, f32[1,1]{1,0:T(1,128)}) fusion(f32[1,7]{1,0:T(1,128)} %param.29), kind=kLoop, calls=%fused_computation.44 | loop fusion | bytes 56 | tf_op jit(solution)/shard_map/slice | solution.py:23
  2.9 5.0 %and_select_fusion.surf_mat = f32[1,12]{1,0:T(1,128)} fusion(f32[]{:T(128)} %bitcast.13, s32[]{:T(128)} %bitcast.12, f32[]{:T(128)} %bitcast.11, s32[]{:T(128)} %bitcast.10, f32[]{:T(128)} %bitcast.9, s32[]{:T(128)} %bitcast.8, f32[]{:T(128)} %bitcast.7, s32[]{:T(128)} %bitcast.6, f32[]{:T(128)} %bitcast.5, s32[]{:T(128)} %bitcast.4, f32[]{:T(128)} %bitcast.3, ...), kind=kLoop, calls=%fused_computation.32 | loop fusion | flops 300 | bytes 108 | tf_op jit(solution)/shard_map/jit(_where)/select_n | solution.py:402
  7.9 0.8 slice_bitcast_fusion.2
  8.7 0.7 broadcast_add_fusion
  9.3 1.3 %select_add_fusion.flux_mat = f32[4,3]{1,0:T(4,128)} fusion(f32[4]{0:T(128)S(1)} %get-tuple-element.19, f32[4]{0:T(128)S(1)} %get-tuple-element.18, s32[3]{0:T(128)S(1)} %iota_add_fusion, s32[4]{0:T(128)S(1)} %broadcast_add_fusion, s32[4]{0:T(128)} %param.26), kind=kLoop, calls=%fused_computation.24 | loop fusion | flops 60 | bytes 124 | tf_op jit(solution)/shard_map/add | solution.py:23
  10.6 0.8 slice_bitcast_fusion
  11.5 0.6 reshape.221.top_ref
  12.1 1.3 %fusion.mean_ref = bf16[1440,360]{1,0:T(8,128)(2,1)} fusion(s32[1440]{0:T(1024)S(1)} %add_select_fusion.1), kind=kLoop, calls=%fused_computation.2 | loop fusion | flops 1036800 | bytes 1042560 | tf_op jit(solution)/shard_map/convert_element_type | solution.py:215
  13.4 1.3 %pad.8.embed_ref = f32[8,1024]{1,0:T(8,128)} pad(f32[4,1024]{1,0:T(4,128)} %param.25, f32[]{:T(128)} %constant.66.clone.1), padding=0_4x0_0 | pad | bytes 49156 | tf_op jit(solution)/shard_map/jit(_pad)/pad | solution.py:216
  14.7 0.7 convert_bitcast_fusion
  15.5 0.0 copy-done
  15.5 0.2 copy.39
  15.7 1.1 pad_maximum_fusion.ocean_ref.mid_ref
  16.8 0.0 copy-start.2
  16.8 64.6 %atmos_block.1 = (bf16[360,1024]{1,0:T(8,128)(2,1)}, bf16[4,16,360]{2,1,0:T(8,128)(2,1)}, bf16[4,16,360]{2,1,0:T(8,128)(2,1)}, bf16[4,16,360]{2,1,0:T(8,128)(2,1...) custom-call(f32[1,12]{1,0:T(1,128)} %and_select_fusion.surf_mat, f32[4,3]{1,0:T(4,128)} %select_add_fusion.flux_mat, ...), custom_call_target="tpu_custom_call" | custom-call | tf_op jit(solution)/shard_map/atmos_block/pallas_call | solution.py:222
  81.4 0.0 copy-start.3
  81.4 0.6 pad_add_fusion.pos_ref
  82.0 1.2 %fusion.1.spread_ref = bf16[360,1536]{1,0:T(8,128)(2,1)} fusion(s32[1536]{0:T(1024)S(1)} %add_select_fusion), kind=kLoop, calls=%fused_computation.3 | loop fusion | flops 1105920 | bytes 1112064 | tf_op jit(solution)/shard_map/convert_element_type | solution.py:354
  83.3 0.0 copy-done.2
  83.3 0.1 copy.32
  83.4 0.1 pad.11.clone
  83.5 0.3 pad_maximum_fusion.1
  83.9 0.9 copy.30.first_ref
  84.8 0.0 copy-done.3
  84.8 0.1 copy.29
  84.9 0.1 pad.9
  85.0 0.7 copy.41
  85.7 30.3 %ocean_steps.1 = bf16[4,76,1440]{2,1,0:T(8,128)(2,1)} custom-call(s32[2]{0:T(128)} %pad_add_fusion.pos_ref, bf16[4,77,1440]{2,1,0:T(8,128)(2,1)} %get-tuple-element.9.low_ref, bf16[4,77,1440]{2,1,0:T(8,128)(2,1)} %pad_maximum_fusion.ocean_ref.mid_ref, bf16[4,77,1440]{2,1,0:T(8,128)(2,1)} %get-tuple-element.10.high_ref, ...), custom_call_target="tpu_custom_call" | custom-call | tf_op jit(solution)/shard_map/ocean_steps/pallas_call | solution.py:358
  116.0 0.0 copy-start.1
  116.0 2.9 %copy.31 = bf16[76,4,1440]{2,1,0:T(4,128)(2,1)} copy(bf16[76,4,1440]{2,0,1:T(8,128)(2,1)} %bitcast.47) | data formatting | bytes 1751040
  118.9 0.0 copy-done.1
  118.9 0.9 copy.44
  (10 shorter events, 0.1 us)
Async XLA Ops:
  0.6 14.8 %copy-start = (bf16[76,4,1440]{2,1,0:T(4,128)(2,1)S(1)}, bf16[76,4,1440]{2,1,0:T(4,128)(2,1)}, u32[]{:S(2)}) copy-start(bf16[76,4,1440]{2,1,0:T(4,128)(2,1)} %param.17) | copy-start | bytes 2626564
  16.8 66.5 %copy-start.2 = (bf16[9,128,92]{1,2,0:T(8,128)(2,1)S(1)}, bf16[9,128,92]{1,2,0:T(8,128)(2,1)}, u32[]{:S(2)}) copy-start(bf16[9,128,92]{1,2,0:T(8,128)(2,1)} %param.30) | copy-start | bytes 635908
  81.4 3.4 %copy-start.3 = (bf16[9,76,128]{2,1,0:T(8,128)(2,1)S(1)}, bf16[9,76,128]{2,1,0:T(8,128)(2,1)}, u32[]{:S(2)}) copy-start(bf16[9,76,128]{2,1,0:T(8,128)(2,1)} %param.31) | copy-start | bytes 525316
  116.0 2.9 %copy-start.1 = (bf16[360,1024]{1,0:T(8,128)(2,1)S(1)}, bf16[360,1024]{1,0:T(8,128)(2,1)}, u32[]{:S(2)}) copy-start(bf16[360,1024]{1,0:T(8,128)(2,1)} %get-tuple-element.29) | copy-start | bytes 2211844

commit v2 on v1

--- a/solution.py
+++ b/solution.py
@@ -15,18 +15,10 @@
     return values * lax.rsqrt(jnp.mean(values * values, axis=-1, keepdims=True) + 1e-06) * scaling
 
 
-def band_matrix(starts, weight, first_col, col_count):
-    columns = first_col + jnp.arange(col_count, dtype=jnp.int32)
-    summed = jnp.zeros((starts.shape[0], col_count), jnp.float32)
-    for offset in range(weight.shape[1]):
-        matches = (columns[None, :] == starts[:, None] + offset).astype(jnp.float32)
-        summed = summed + weight[:, offset : offset + 1] * matches
-    return summed
-
-
-def atmos_kernel(surf_mat, flux_mat, scale_ref, atmos_ref, top_ref, mean_ref, embed_ref, gain_ref,
-                 flux_gain_ref, qkv_ref, wout_ref, wflux_ref, ocean_ref,
-                 after_ref, flux_mid, flux_low, flux_high, ocean_low, ocean_high,
+def atmos_kernel(surf_first, surf_weight, flux_first, flux_weight, scale_ref, atmos_ref, top_ref,
+                 embed_ref, gain_ref, flux_gain_ref, qkv_ref, wout_ref, wflux_ref, ocean_ref,
+                 land_ref,
+                 after_ref, flux_mid, flux_low, flux_high, ocean_low, ocean_high, land_low, land_high,
                  surf, near, near_q, near_k, near_v, held, rows, send_sems, recv_sems):
     me = lax.axis_index("lat")
     count = lax.axis_size("lat")
@@ -91,8 +83,13 @@
         rows[2] = jnp.zeros_like(rows[2])
         flux_high[...] = jnp.zeros_like(flux_high)
 
+    olon = top_ref.shape[1]
+    alon = olon // SPAN
+    spans = lax.broadcasted_iota(jnp.int32, (olon, alon), 0) // SPAN
+    chosen = spans == lax.broadcasted_iota(jnp.int32, (olon, alon), 1)
+    mean = jnp.where(chosen, 1.0, 0.0).astype(jnp.bfloat16)
     surf[1] = (
-        jnp.dot(top_ref[...], mean_ref[...], preferred_element_type=jnp.float32) * (1.0 / SPAN)
+        jnp.dot(top_ref[...], mean, preferred_element_type=jnp.float32) * (1.0 / SPAN)
     ).astype(jnp.bfloat16)
     pl.semaphore_wait(barrier, jnp.where(has[0], 1, 0) + jnp.where(has[1], 1, 0))
     surf_args = (0, surf.at[1], surf.at[2], surf.at[0])
@@ -102,19 +99,25 @@
     for part in range(3):
         block = surf[part].astype(jnp.float32)
         for i in range(block.shape[0] // VARS):
-            weight = surf_mat[0, part * (block.shape[0] // VARS) + i]
+            rows_here = block.shape[0] // VARS
+            column = (me + part - 1) * rows_here + i
+            weight = jnp.float32(0.0)
+            for b in range(surf_weight.shape[1]):
+                weight = weight + jnp.where(surf_first[0] + b == column, surf_weight[0, b], 0.0)
+            weight = jnp.where((column >= 0) & (column < count * rows_here), weight, 0.0)
             band = band + weight * block[i * VARS : (i + 1) * VARS]
     band = jnp.concatenate([band, jnp.zeros_like(band)], axis=0)
+    embed = jnp.concatenate([embed_ref[...], jnp.zeros_like(embed_ref[...])], axis=0)
     started = atmos_ref[...].astype(jnp.float32) + lax.dot_general(
-        band, embed_ref[...], (((0,), (0,)), ((), ())), precision=lax.Precision.HIGHEST,
+        band, embed, (((0,), (0,)), ((), ())), precision=lax.Precision.HIGHEST,
         preferred_element_type=jnp.float32,
     )
     held[...] = started
     near[1] = rms_norm(started, gain_ref[...]).astype(jnp.bfloat16)
     near_args = (1, near.at[1], near.at[2], near.at[0])
     ocean_args = (2, ocean_ref, ocean_high, ocean_low)
+    land_args = (5, land_ref, land_high, land_low)
     start_both(*near_args)
-    start_both(*ocean_args)
 
     lane = lax.broadcasted_iota(jnp.int32, (1, group), 1) // depth
 
@@ -145,6 +148,8 @@
 
     lax.fori_loop(0, groups, own, 0)
     wait_both(*near_args)
+    start_both(*ocean_args)
+    start_both(*land_args)
 
     def attend(g, carry):
         column = g * group
@@ -194,39 +199,42 @@
     wait_both(*rows_args)
     sources = [rows[part].astype(jnp.float32) for part in range(3)]
     for i in range(flux_mid.shape[0]):
-        flux_mid[i] = (
-            flux_mat[i, 0] * sources[0] + flux_mat[i, 1] * sources[1] + flux_mat[i, 2] * sources[2]
-        ).astype(jnp.bfloat16)
+        regridded = jnp.zeros_like(sources[0])
+        for part in range(3):
+            weight = jnp.float32(0.0)
+            for b in range(flux_weight.shape[1]):
+                weight = weight + jnp.where(flux_first[i] + b == me + part - 1, flux_weight[i, b], 0.0)
+            regridded = regridded + weight * sources[part]
+        flux_mid[i] = regridded.astype(jnp.bfloat16)
     flux_args = (4, flux_mid, flux_high, flux_low)
     start_both(*flux_args)
     wait_both(*ocean_args)
+    wait_both(*land_args)
     wait_both(*flux_args)
 
 
-def atmos_block(surf_mat, flux_mat, head_scale, atmos, top, gain_attn, gain_flux, w_qkv, w_out,
-                w_flux, surf_embed, packed):
+def atmos_block(surf_start, surf_weight, flux_start, flux_weight, head_scale, atmos, top, gain_attn,
+                gain_flux, w_qkv, w_out, w_flux, surf_embed, ocean, land_mask):
     token_count, width = atmos.shape
     alon = top.shape[1] // SPAN
-    orows = packed.shape[0]
+    orows = ocean.shape[0]
     nflux = w_flux.shape[1]
     group = 256
     groups = width // group
-    index = jnp.arange(top.shape[1], dtype=jnp.int32) // SPAN
-    mean = (index[:, None] == jnp.arange(alon, dtype=jnp.int32)[None, :]).astype(jnp.bfloat16)
-    embed = jnp.pad(surf_embed, ((0, VARS), (0, 0)))
     vmem = pl.BlockSpec(memory_space=pltpu.VMEM)
     smem = pl.BlockSpec(memory_space=pltpu.SMEM)
     anywhere = pl.BlockSpec(memory_space=pl.ANY)
     flux_shape = jax.ShapeDtypeStruct((orows, nflux, alon), jnp.bfloat16)
-    ocean_shape = jax.ShapeDtypeStruct(packed.shape, packed.dtype)
+    ocean_shape = jax.ShapeDtypeStruct(ocean.shape, ocean.dtype)
+    land_shape = jax.ShapeDtypeStruct(land_mask.shape, land_mask.dtype)
     return pl.pallas_call(
         atmos_kernel,
         out_shape=[
             jax.ShapeDtypeStruct((token_count, width), jnp.bfloat16),
-            flux_shape, flux_shape, flux_shape, ocean_shape, ocean_shape,
+            flux_shape, flux_shape, flux_shape, ocean_shape, ocean_shape, land_shape, land_shape,
         ],
-        in_specs=[smem] * 3 + [vmem] * 9 + [anywhere],
-        out_specs=[vmem] * 4 + [anywhere] * 2,
+        in_specs=[smem] * 5 + [vmem] * 8 + [anywhere] * 2,
+        out_specs=[vmem] * 4 + [anywhere] * 4,
         scratch_shapes=[
             pltpu.VMEM((3, top.shape[0], alon), jnp.bfloat16),
             pltpu.VMEM((3, token_count, width), jnp.bfloat16),
@@ -235,21 +243,21 @@
             pltpu.VMEM((groups, 3, token_count, group), jnp.bfloat16),
             pltpu.VMEM((token_count, width), jnp.float32),
             pltpu.VMEM((3, nflux, alon), jnp.bfloat16),
-            pltpu.SemaphoreType.DMA((5, 2)),
-            pltpu.SemaphoreType.DMA((5, 2)),
+            pltpu.SemaphoreType.DMA((6, 2)),
+            pltpu.SemaphoreType.DMA((6, 2)),
         ],
         compiler_params=pltpu.CompilerParams(
             collective_id=0, has_side_effects=True, vmem_limit_bytes=58 * 1024 * 1024
         ),
         name="atmos_block",
-    )(surf_mat, flux_mat, head_scale, atmos, top, mean, embed, gain_attn[None, :],
-      gain_flux[None, :], w_qkv, w_out, w_flux.T, packed)
-
-
-def ocean_kernel(pos_ref, low_ref, mid_ref, high_ref,
-                 flux_low, flux_mid, flux_high, spread_ref,
+    )(surf_start, surf_weight, flux_start, flux_weight, head_scale, atmos, top, surf_embed,
+      gain_attn[None, :], gain_flux[None, :], w_qkv, w_out, w_flux.T, ocean, land_mask)
+
+
+def ocean_kernel(low_ref, mid_ref, high_ref, land_low, land_mid, land_high,
+                 flux_low, flux_mid, flux_high,
                  first_ref, second_ref, out_ref, xs, hs, st, sea):
-    och = mid_ref.shape[1] - 1
+    och = mid_ref.shape[1]
     olon = mid_ref.shape[2]
     orows = mid_ref.shape[0]
     wide = xs.shape[1]
@@ -257,8 +265,13 @@
     hid = first_ref.shape[0] // 3
     opad = second_ref.shape[0] // 3
     stride = opad + nflux
-    first_row = pos_ref[0]
-    total = pos_ref[1]
+    first_row = lax.axis_index("lat") * orows
+    total = lax.axis_size("lat") * orows
+    alon = flux_mid.shape[2]
+    column = lax.broadcasted_iota(jnp.int32, (alon, wide), 1)
+    longitude = jnp.where(column < olon, column, jnp.where(column == olon, 0, olon - 1))
+    chosen = longitude // SPAN == lax.broadcasted_iota(jnp.int32, (alon, wide), 0)
+    repeat = jnp.where(chosen, 1.0, 0.0).astype(jnp.bfloat16)
     tail = wide - 128
     first_pad = olon - tail
 
@@ -273,17 +286,19 @@
         right = pltpu.roll(full[2 * size : 3 * size], wide - 1, 1)
         return left + full[size : 2 * size] + right
 
-    sides = ((low_ref, flux_low), (mid_ref, flux_mid), (high_ref, flux_high))
-    for part, (ref, flux) in enumerate(sides):
-        def fill(i, carry, ref=ref, flux=flux, part=part):
+    sides = (
+        (low_ref, land_low, flux_low), (mid_ref, land_mid, flux_mid), (high_ref, land_high, flux_high)
+    )
+    for part, (ref, land, flux) in enumerate(sides):
+        def fill(i, carry, ref=ref, land=land, flux=flux, part=part):
             row = part * orows + i
             place = first_row + row - orows
-            packed = ref[i].astype(jnp.float32)
-            packed = jnp.where((place >= 0) & (place < total), packed, 0.0)
-            state = packed[0:och]
-            sea[row, :, 0:tail] = packed[och:, 0:tail]
+            inside = (place >= 0) & (place < total)
+            state = jnp.where(inside, ref[i].astype(jnp.float32), 0.0)
+            cells = jnp.where(inside, land[pl.ds(i, 1), :].astype(jnp.float32), 0.0)
+            sea[row, :, 0:tail] = cells[:, 0:tail]
             sea[row, :, tail:] = jnp.concatenate(
-                [packed[och:, tail:], jnp.zeros((1, wide - olon), jnp.float32)], axis=1
+                [cells[:, tail:], jnp.zeros((1, wide - olon), jnp.float32)], axis=1
             )
             state = jnp.concatenate([state, jnp.zeros((opad - och, olon), jnp.float32)], axis=0)
             last = jnp.concatenate(
@@ -293,7 +308,7 @@
             st[row, :, tail:] = wrap(state[:, 0:128], last)
             base = pl.multiple_of(row * stride, 16)
             xs[pl.ds(base, opad), :] = st[row].astype(jnp.bfloat16)
-            spread = jnp.dot(flux[i], spread_ref[...], preferred_element_type=jnp.float32)
+            spread = jnp.dot(flux[i], repeat, preferred_element_type=jnp.float32)
             base = pl.multiple_of(row * stride + opad, 16)
             xs[pl.ds(base, nflux), :] = spread.astype(jnp.bfloat16)
             return carry
@@ -313,7 +328,7 @@
             hs[pl.ds(base, hid), 0:tail] = hidden[:, 0:tail].astype(jnp.bfloat16)
             hs[pl.ds(base, hid), tail:] = wrap(hidden[:, 0:128], hidden[:, tail:]).astype(jnp.bfloat16)
             return carry
-        lax.fori_loop(edge, 3 * orows - edge, first, 0)
+        lax.fori_loop(edge, 3 * orows - edge, first, 0, unroll=2)
 
         def second(row, carry):
             block = hs[pl.ds(pl.multiple_of((row - 1) * hid, 16), 3 * hid), :]
@@ -327,21 +342,20 @@
                 base = pl.multiple_of(row * stride, 16)
                 xs[pl.ds(base, opad), :] = st[row].astype(jnp.bfloat16)
             return carry
-        lax.fori_loop(edge + 1, 3 * orows - edge - 1, second, 0)
+        lax.fori_loop(edge + 1, 3 * orows - edge - 1, second, 0, unroll=2)
 
 
 def round_up(value, unit):
     return (value + unit - 1) // unit * unit
 
 
-def ocean_steps(state_parts, fluxes, conv_first, conv_second, position, band_count):
+def ocean_steps(state_parts, land_parts, fluxes, conv_first, conv_second):
     orows, _, olon = state_parts[1].shape
     och = conv_second.shape[1]
     nflux = fluxes[1].shape[1]
     hid = conv_first.shape[1]
     opad = round_up(och, 16)
     wide = round_up(olon + 2, 128)
-    alon = fluxes[1].shape[2]
     first = conv_first.reshape(3, 3, hid, och + nflux)
     first = jnp.concatenate(
         [first[..., :och], jnp.zeros((3, 3, hid, opad - och), first.dtype), first[..., och:]], axis=3
@@ -349,16 +363,11 @@
     first = first.transpose(1, 2, 0, 3).reshape(3 * hid, 3 * (opad + nflux))
     second = jnp.pad(conv_second.reshape(3, 3, och, hid), ((0, 0), (0, 0), (0, opad - och), (0, 0)))
     second = second.transpose(1, 2, 0, 3).reshape(3 * opad, 3 * hid)
-    column = jnp.arange(wide, dtype=jnp.int32)
-    longitude = jnp.where(column < olon, column, jnp.where(column == olon, 0, olon - 1))
-    spread = (longitude[None, :] // SPAN == jnp.arange(alon, dtype=jnp.int32)[:, None]).astype(jnp.bfloat16)
-    scalars = jnp.stack([position * orows, band_count * orows]).astype(jnp.int32)
     vmem = pl.BlockSpec(memory_space=pltpu.VMEM)
-    smem = pl.BlockSpec(memory_space=pltpu.SMEM)
     return pl.pallas_call(
         ocean_kernel,
         out_shape=jax.ShapeDtypeStruct((orows, och, olon), jnp.bfloat16),
-        in_specs=[smem] + [vmem] * 9,
+        in_specs=[vmem] * 11,
         out_specs=vmem,
         scratch_shapes=[
             pltpu.VMEM((3 * orows * (opad + nflux), wide), jnp.bfloat16),
@@ -368,7 +377,7 @@
         ],
         compiler_params=pltpu.CompilerParams(vmem_limit_bytes=60 * 1024 * 1024),
         name="ocean_steps",
-    )(scalars, *state_parts, *fluxes, spread, first, second)
+    )(*state_parts, *land_parts, *fluxes, first, second)
 
 
 def local(
@@ -389,25 +398,17 @@
     conv_first,
     conv_second,
 ):
-    position = lax.axis_index("lat")
-    band_count = lax.axis_size("lat")
     orows = ocean_state.shape[1]
-    packed = jnp.concatenate(
-        [ocean_state.transpose(1, 0, 2), land_mask.astype(jnp.bfloat16)[:, None, :]], axis=1
-    )
+    ocean = ocean_state.transpose(1, 0, 2)
     top = ocean_state[::LEVELS].transpose(1, 0, 2).reshape(orows * VARS, -1)
-    first_column = (position - 1) * orows
-    surf_mat = band_matrix(surf_start, surf_weight, first_column, 3 * orows)
-    columns = first_column + jnp.arange(3 * orows, dtype=jnp.int32)
-    surf_mat = jnp.where((columns >= 0) & (columns < band_count * orows), surf_mat, 0.0)
-    flux_mat = band_matrix(flux_start, flux_weight, position - 1, 3)
-    atmos_next, flux_mid, flux_low, flux_high, ocean_low, ocean_high = atmos_block(
-        surf_mat, flux_mat, head_scale, atmos, top, gain_attn, gain_flux, w_qkv, w_out, w_flux,
-        surf_embed, packed,
-    )
+    outs = atmos_block(
+        surf_start, surf_weight, flux_start, flux_weight, head_scale, atmos, top, gain_attn,
+        gain_flux, w_qkv, w_out, w_flux, surf_embed, ocean, land_mask,
+    )
+    atmos_next, flux_mid, flux_low, flux_high, ocean_low, ocean_high, land_low, land_high = outs
     ocean_next = ocean_steps(
-        [ocean_low, packed, ocean_high], [flux_low, flux_mid, flux_high], conv_first, conv_second,
-        position, band_count,
+        [ocean_low, ocean, ocean_high], [land_low, land_mask, land_high],
+        [flux_low, flux_mid, flux_high], conv_first, conv_second,
     )
     return (atmos_next, ocean_next.transpose(1, 0, 2))
 

time: 120 us -> 103 us (0.86)
  other arithmetic: 12.3 us -> 0.35 us
  Pallas kernels: 94.9 us -> 90.2 us
    select_n x3 -> x0, other arithmetic: 5.02 us -> none  [the longest x1 5.01 us: local(): jnp.where((columns >= 0) & (columns < band_count * orows), surf_mat, 0.0)]
    pallas_call x1, Pallas kernels: 30.3 us -> 25.5 us  [ocean_steps(): pl.pallas_call(ocean_kernel, out_shape=jax.ShapeDtypeStruct((orows, och,...]
    unnamed x15 -> x14, local copies, waits for them, and re-layouts: 4.81 us -> 8.22 us
    convert_element_type x2 -> x0, other arithmetic: 2.47 us -> none  [the longest x1 1.25 us: atmos_block(): (index[:, None] == jnp.arange(alon, dtype=jnp.int32)[None, :]).astype(jnp...]
    add x3 -> x0, other arithmetic: 1.96 us -> none  [the longest x1 1.3 us: band_matrix(): summed = summed + weight[:, offset:offset + 1] * matches]
    slice x1 -> x0, local copies, waits for them, and re-layouts: 1.59 us -> none  [band_matrix(): summed = summed + weight[:, offset:offset + 1] * matches]
    pad x1 -> x0, local copies, waits for them, and re-layouts: 1.34 us -> none  [atmos_block(): embed = jnp.pad(surf_embed, ((0, VARS), (0, 0)))]
where the time goes in v2:
time: 103 us
  Pallas kernels  90.2 us (88%)
  local copies, waits for them, and re-layouts  10.9 us (11%)
  between operations  1.43 us (1%)
    pallas_call x1, Pallas kernels, atmos_block(): pl.pallas_call(atmos_kernel, out_shape=[jax.ShapeDtypeStruct((token_count...  64.6 us
    pallas_call x1, Pallas kernels, ocean_steps(): pl.pallas_call(ocean_kernel, out_shape=jax.ShapeDtypeStruct((orows, och,...  25.5 us
    unnamed x14, local copies, waits for them, and re-layouts  8.22 us

profile of v2, /device:TPU:9, one launch (start us, length us, event | category | flops | bytes accessed | tf_op | source)
XLA Modules:
  0.0 102.8 jit_solution(17814137600804926336)
XLA Ops:
  0.6 0.0 copy-start.1
  1.3 1.3 %copy.27.flux_weight = f32[4,2]{1,0:T(4,128)} copy(f32[4,2]{0,1:T(2,128)} %param.27) | data formatting | bytes 64 | tf_op args[11]
  2.7 0.8 slice_bitcast_fusion
  3.5 0.6 reshape.19.top_ref
  4.2 2.3 %copy.40 = bf16[76,4,1440]{2,0,1:T(8,128)(2,1)} copy(bf16[76,4,1440]{2,1,0:T(4,128)(2,1)} %param.17) | data formatting | bytes 1751040 | tf_op args[1]
  6.5 0.0 copy-start.2
  6.5 64.6 %atmos_block.1 = (bf16[360,1024]{1,0:T(8,128)(2,1)}, bf16[4,16,360]{2,1,0:T(8,128)(2,1)}, bf16[4,16,360]{2,1,0:T(8,128)(2,1)}, bf16[4,16,360]{2,1,0:T(8,128)(2,1...) custom-call(s32[1]{0:T(128)S(6)} %copy.44.surf_first, ...), custom_call_target="tpu_custom_call" | custom-call | tf_op jit(solution)/shard_map/atmos_block/pallas_call | solution.py:230
  71.1 0.0 copy-start
  71.1 0.0 copy-done.1
  71.2 0.1 copy.33
  71.3 0.1 pad.6.clone
  71.4 0.3 pad_maximum_fusion
  71.8 0.9 copy.31.first_ref
  72.7 0.0 copy-done.2
  72.7 0.1 copy.30
  72.8 0.1 pad.4
  72.9 0.7 copy.42
  73.6 25.5 %ocean_steps.1 = bf16[4,76,1440]{2,1,0:T(8,128)(2,1)} custom-call(bf16[4,76,1440]{2,1,0:T(8,128)(2,1)} %get-tuple-element.11.low_ref, bf16[4,76,1440]{2,1,0:T(8,128)(2,1)} %bitcast.26, bf16[4,76,1440]{2,1,0:T(8,128)(2,1)} %get-tuple-element.12.high_ref, s32[4,1440]{1,0:T(4,128)} %get-tuple-element.13.land_low, s32[4,1440]{1,0:T(4,128)} %land_mid.1, ...), custom_call_target="tpu_custom_call" | custom-call | tf_op jit(solution)/shard_map/ocean_steps/pallas_call | solution.py:367
  99.1 2.9 %copy.32 = bf16[76,4,1440]{2,1,0:T(4,128)(2,1)} copy(bf16[76,4,1440]{2,0,1:T(8,128)(2,1)} %bitcast.27) | data formatting | bytes 1751040
  102.0 0.0 copy-done
  102.0 0.9 copy.45
  (6 shorter events, 0.1 us)
Async XLA Ops:
  0.6 70.5 %copy-start.1 = (bf16[9,128,92]{1,2,0:T(8,128)(2,1)S(1)}, bf16[9,128,92]{1,2,0:T(8,128)(2,1)}, u32[]{:S(2)}) copy-start(bf16[9,128,92]{1,2,0:T(8,128)(2,1)} %param.30) | copy-start | bytes 635908
  6.5 66.2 %copy-start.2 = (bf16[9,76,128]{2,1,0:T(8,128)(2,1)S(1)}, bf16[9,76,128]{2,1,0:T(8,128)(2,1)}, u32[]{:S(2)}) copy-start(bf16[9,76,128]{2,1,0:T(8,128)(2,1)} %param.31) | copy-start | bytes 525316
  71.1 30.9 %copy-start = (bf16[360,1024]{1,0:T(8,128)(2,1)S(1)}, bf16[360,1024]{1,0:T(8,128)(2,1)}, u32[]{:S(2)}) copy-start(bf16[360,1024]{1,0:T(8,128)(2,1)} %get-tuple-element.24) | copy-start | bytes 2211844

commit v3 on v2

--- a/solution.py
+++ b/solution.py
@@ -19,7 +19,8 @@
                  embed_ref, gain_ref, flux_gain_ref, qkv_ref, wout_ref, wflux_ref, ocean_ref,
                  land_ref,
                  after_ref, flux_mid, flux_low, flux_high, ocean_low, ocean_high, land_low, land_high,
-                 surf, near, near_q, near_k, near_v, held, rows, send_sems, recv_sems):
+                 surf, near, near_q, near_k, near_v, own_mixed, own_largest, own_total, held, rows,
+                 qkv_here, wout_here, load_sems, send_sems, recv_sems):
     me = lax.axis_index("lat")
     count = lax.axis_size("lat")
     token_count, width = atmos_ref.shape
@@ -60,6 +61,12 @@
             send(kind, 0, source, to_high).wait_recv()
             send(kind, 1, source, to_low).wait_send()
 
+    loads = (
+        pltpu.make_async_copy(qkv_ref, qkv_here, load_sems.at[0]),
+        pltpu.make_async_copy(wout_ref, wout_here, load_sems.at[1]),
+    )
+    for load in loads:
+        load.start()
     barrier = pltpu.get_barrier_semaphore()
     for side in range(2):
         @pl.when(has[side])
@@ -131,8 +138,14 @@
 
     def project(part, column):
         return jnp.dot(
-            near[part], qkv_ref[:, pl.ds(pl.multiple_of(column, group), group)],
+            near[part], qkv_here[:, pl.ds(pl.multiple_of(column, group), group)],
             preferred_element_type=jnp.float32,
+        )
+
+    def head_scores(queries, h, keys):
+        query = jnp.where(lane == h, queries, jnp.zeros_like(queries))
+        return lax.dot_general(
+            query, keys, (((1,), (1,)), ((), ())), preferred_element_type=jnp.float32
         )
 
     def own(g, carry):
@@ -144,9 +157,24 @@
         near_q[g] = (query * (scale * (1.0 / depth**0.5))).astype(jnp.bfloat16)
         near_k[g, 1] = head_scales(project(1, width + column)).astype(jnp.bfloat16)
         near_v[g, 1] = project(1, 2 * width + column).astype(jnp.bfloat16)
+        queries = near_q[g]
+        mixed = jnp.zeros((token_count, group), jnp.float32)
+        for h in range(per_group):
+            score = head_scores(queries, h, near_k[g, 1])
+            largest = jnp.max(score, axis=1, keepdims=True)
+            raised = jnp.exp(score - largest)
+            own_largest[g * per_group + h] = largest
+            own_total[g * per_group + h] = jnp.sum(raised, axis=1, keepdims=True)
+            value = jnp.dot(
+                raised.astype(jnp.bfloat16), near_v[g, 1], preferred_element_type=jnp.float32
+            )
+            mixed = jnp.where(lane == h, value, mixed)
+        own_mixed[g] = mixed
         return carry
 
+    loads[0].wait()
     lax.fori_loop(0, groups, own, 0)
+    loads[1].wait()
     wait_both(*near_args)
     start_both(*ocean_args)
     start_both(*land_args)
@@ -159,30 +187,25 @@
         queries = near_q[g]
         mixed = jnp.zeros((token_count, group), jnp.float32)
         for h in range(per_group):
-            query = jnp.where(lane == h, queries, jnp.zeros_like(queries))
-            scores = []
-            for part in range(3):
-                score = lax.dot_general(
-                    query, near_k[g, part], (((1,), (1,)), ((), ())),
-                    preferred_element_type=jnp.float32,
-                )
-                if part != 1:
-                    score = jnp.where(has[part // 2], score, -1e30)
-                scores.append(score)
-            largest = jnp.max(jnp.maximum(jnp.maximum(scores[0], scores[1]), scores[2]),
-                              axis=1, keepdims=True)
-            raised = [jnp.exp(score - largest) for score in scores]
-            total = jnp.sum(raised[0] + raised[1] + raised[2], axis=1, keepdims=True)
-            inverse = 1.0 / total
-            value = jnp.zeros((token_count, group), jnp.float32)
-            for part in range(3):
-                value = value + jnp.dot(
-                    (raised[part] * inverse).astype(jnp.bfloat16), near_v[g, part],
-                    preferred_element_type=jnp.float32,
-                )
+            low = jnp.where(has[0], head_scores(queries, h, near_k[g, 0]), -1e30)
+            high = jnp.where(has[1], head_scores(queries, h, near_k[g, 2]), -1e30)
+            before = own_largest[g * per_group + h]
+            largest = jnp.maximum(
+                jnp.max(jnp.maximum(low, high), axis=1, keepdims=True), before
+            )
+            low = jnp.exp(low - largest)
+            high = jnp.exp(high - largest)
+            fade = jnp.exp(before - largest)
+            total = own_total[g * per_group + h] * fade + jnp.sum(low + high, axis=1, keepdims=True)
+            value = jnp.dot(
+                low.astype(jnp.bfloat16), near_v[g, 0], preferred_element_type=jnp.float32
+            ) + jnp.dot(
+                high.astype(jnp.bfloat16), near_v[g, 2], preferred_element_type=jnp.float32
+            )
+            value = (own_mixed[g] * fade + value) * (1.0 / total)
             mixed = jnp.where(lane == h, value, mixed)
         held[...] += jnp.dot(
-            mixed.astype(jnp.bfloat16), wout_ref[pl.ds(pl.multiple_of(column, group), group), :],
+            mixed.astype(jnp.bfloat16), wout_here[pl.ds(pl.multiple_of(column, group), group), :],
             preferred_element_type=jnp.float32,
         )
         return carry
@@ -233,7 +256,7 @@
             jax.ShapeDtypeStruct((token_count, width), jnp.bfloat16),
             flux_shape, flux_shape, flux_shape, ocean_shape, ocean_shape, land_shape, land_shape,
         ],
-        in_specs=[smem] * 5 + [vmem] * 8 + [anywhere] * 2,
+        in_specs=[smem] * 5 + [vmem] * 5 + [anywhere] * 2 + [vmem] + [anywhere] * 2,
         out_specs=[vmem] * 4 + [anywhere] * 4,
         scratch_shapes=[
             pltpu.VMEM((3, top.shape[0], alon), jnp.bfloat16),
@@ -241,8 +264,14 @@
             pltpu.VMEM((groups, token_count, group), jnp.bfloat16),
             pltpu.VMEM((groups, 3, token_count, group), jnp.bfloat16),
             pltpu.VMEM((groups, 3, token_count, group), jnp.bfloat16),
+            pltpu.VMEM((groups, token_count, group), jnp.float32),
+            pltpu.VMEM((head_scale.shape[0], token_count, 1), jnp.float32),
+            pltpu.VMEM((head_scale.shape[0], token_count, 1), jnp.float32),
             pltpu.VMEM((token_count, width), jnp.float32),
             pltpu.VMEM((3, nflux, alon), jnp.bfloat16),
+            pltpu.VMEM(w_qkv.shape, w_qkv.dtype),
+            pltpu.VMEM(w_out.shape, w_out.dtype),
+            pltpu.SemaphoreType.DMA((2,)),
             pltpu.SemaphoreType.DMA((6, 2)),
             pltpu.SemaphoreType.DMA((6, 2)),
         ],

time: 103 us -> 100 us (0.971)
  Pallas kernels: 90.2 us -> 87.5 us
    pallas_call x1, Pallas kernels: 64.6 us -> 61.8 us  [atmos_block(): pl.pallas_call(atmos_kernel, out_shape=[jax.ShapeDtypeStruct((token_count...]
where the time goes in v3:
time: 100 us
  Pallas kernels  87.5 us (88%)
  local copies, waits for them, and re-layouts  10.9 us (11%)
  between operations  1.43 us (1%)
    pallas_call x1, Pallas kernels, atmos_block(): pl.pallas_call(atmos_kernel, out_shape=[jax.ShapeDtypeStruct((token_count...  61.8 us
    pallas_call x1, Pallas kernels, ocean_steps(): pl.pallas_call(ocean_kernel, out_shape=jax.ShapeDtypeStruct((orows, och,...  25.7 us
    unnamed x14, local copies, waits for them, and re-layouts  8.22 us

profile of v3, /device:TPU:9, one launch (start us, length us, event | category | flops | bytes accessed | tf_op | source)
XLA Modules:
  0.0 100.1 jit_solution(464490436284598840)
XLA Ops:
  0.6 0.0 copy-start.1
  1.3 1.3 %copy.27.flux_weight = f32[4,2]{1,0:T(4,128)} copy(f32[4,2]{0,1:T(2,128)} %param.27) | data formatting | bytes 64 | tf_op args[11]
  2.7 0.8 slice_bitcast_fusion
  3.5 0.6 reshape.19.top_ref
  4.2 2.3 %copy.40 = bf16[76,4,1440]{2,0,1:T(8,128)(2,1)} copy(bf16[76,4,1440]{2,1,0:T(4,128)(2,1)} %param.17) | data formatting | bytes 1751040 | tf_op args[1]
  6.5 0.0 copy-start.2
  6.5 61.8 %atmos_block.1 = (bf16[360,1024]{1,0:T(8,128)(2,1)}, bf16[4,16,360]{2,1,0:T(8,128)(2,1)}, bf16[4,16,360]{2,1,0:T(8,128)(2,1)}, bf16[4,16,360]{2,1,0:T(8,128)(2,1...) custom-call(s32[1]{0:T(128)S(6)} %copy.44.surf_first, ...), custom_call_target="tpu_custom_call" | custom-call | tf_op jit(solution)/shard_map/atmos_block/pallas_call | solution.py:253
  68.2 0.0 copy-start
  68.2 0.0 copy-done.1
  68.3 0.1 copy.33
  68.4 0.1 pad.6.clone
  68.5 0.3 pad_maximum_fusion
  68.9 0.9 copy.31.first_ref
  69.8 0.0 copy-done.2
  69.8 0.1 copy.30
  69.9 0.1 pad.4
  70.0 0.7 copy.42
  70.7 25.7 %ocean_steps.1 = bf16[4,76,1440]{2,1,0:T(8,128)(2,1)} custom-call(bf16[4,76,1440]{2,1,0:T(8,128)(2,1)} %get-tuple-element.11.low_ref, bf16[4,76,1440]{2,1,0:T(8,128)(2,1)} %bitcast.26, bf16[4,76,1440]{2,1,0:T(8,128)(2,1)} %get-tuple-element.12.high_ref, s32[4,1440]{1,0:T(4,128)} %get-tuple-element.13.land_low, s32[4,1440]{1,0:T(4,128)} %land_mid.1, ...), custom_call_target="tpu_custom_call" | custom-call | tf_op jit(solution)/shard_map/ocean_steps/pallas_call | solution.py:396
  96.4 2.9 %copy.32 = bf16[76,4,1440]{2,1,0:T(4,128)(2,1)} copy(bf16[76,4,1440]{2,0,1:T(8,128)(2,1)} %bitcast.27) | data formatting | bytes 1751040
  99.3 0.0 copy-done
  99.3 0.9 copy.45
  (6 shorter events, 0.1 us)
Async XLA Ops:
  0.6 67.6 %copy-start.1 = (bf16[9,128,92]{1,2,0:T(8,128)(2,1)S(1)}, bf16[9,128,92]{1,2,0:T(8,128)(2,1)}, u32[]{:S(2)}) copy-start(bf16[9,128,92]{1,2,0:T(8,128)(2,1)} %param.30) | copy-start | bytes 635908
  6.5 63.3 %copy-start.2 = (bf16[9,76,128]{2,1,0:T(8,128)(2,1)S(1)}, bf16[9,76,128]{2,1,0:T(8,128)(2,1)}, u32[]{:S(2)}) copy-start(bf16[9,76,128]{2,1,0:T(8,128)(2,1)} %param.31) | copy-start | bytes 525316
  68.2 31.0 %copy-start = (bf16[360,1024]{1,0:T(8,128)(2,1)S(1)}, bf16[360,1024]{1,0:T(8,128)(2,1)}, u32[]{:S(2)}) copy-start(bf16[360,1024]{1,0:T(8,128)(2,1)} %get-tuple-element.24) | copy-start | bytes 2211844

commit v4 on v3

--- a/solution.py
+++ b/solution.py
@@ -371,7 +371,7 @@
                 base = pl.multiple_of(row * stride, 16)
                 xs[pl.ds(base, opad), :] = st[row].astype(jnp.bfloat16)
             return carry
-        lax.fori_loop(edge + 1, 3 * orows - edge - 1, second, 0, unroll=2)
+        lax.fori_loop(edge + 1, 3 * orows - edge - 1, second, 0, unroll=4)
 
 
 def round_up(value, unit):

time: 100 us -> 99.6 us (level)
  no operation moved by 1% of the time
where the time goes in v4:
time: 99.6 us; the launch traced here: 99.3 us
  Pallas kernels  86.7 us (87%)
  local copies, waits for them, and re-layouts  10.9 us (11%)
  between operations  1.43 us (1%)
    pallas_call x1, Pallas kernels, atmos_block(): pl.pallas_call(atmos_kernel, out_shape=[jax.ShapeDtypeStruct((token_count...  61.8 us
    pallas_call x1, Pallas kernels, ocean_steps(): pl.pallas_call(ocean_kernel, out_shape=jax.ShapeDtypeStruct((orows, och,...  24.9 us
    unnamed x14, local copies, waits for them, and re-layouts  8.22 us

profile of v4, /device:TPU:9, one launch (start us, length us, event | category | flops | bytes accessed | tf_op | source)
XLA Modules:
  0.0 99.3 jit_solution(7969311225356540643)
XLA Ops:
  0.6 0.0 copy-start.1
  1.3 1.3 %copy.27.flux_weight = f32[4,2]{1,0:T(4,128)} copy(f32[4,2]{0,1:T(2,128)} %param.27) | data formatting | bytes 64 | tf_op args[11]
  2.7 0.8 slice_bitcast_fusion
  3.5 0.6 reshape.19.top_ref
  4.2 2.3 %copy.40 = bf16[76,4,1440]{2,0,1:T(8,128)(2,1)} copy(bf16[76,4,1440]{2,1,0:T(4,128)(2,1)} %param.17) | data formatting | bytes 1751040 | tf_op args[1]
  6.5 0.0 copy-start.2
  6.5 61.8 %atmos_block.1 = (bf16[360,1024]{1,0:T(8,128)(2,1)}, bf16[4,16,360]{2,1,0:T(8,128)(2,1)}, bf16[4,16,360]{2,1,0:T(8,128)(2,1)}, bf16[4,16,360]{2,1,0:T(8,128)(2,1...) custom-call(s32[1]{0:T(128)S(6)} %copy.44.surf_first, ...), custom_call_target="tpu_custom_call" | custom-call | tf_op jit(solution)/shard_map/atmos_block/pallas_call | solution.py:253
  68.2 0.0 copy-start
  68.2 0.0 copy-done.1
  68.3 0.1 copy.33
  68.4 0.1 pad.6.clone
  68.5 0.3 pad_maximum_fusion
  68.9 0.9 copy.31.first_ref
  69.8 0.0 copy-done.2
  69.8 0.1 copy.30
  69.9 0.1 pad.4
  70.0 0.7 copy.42
  70.7 24.9 %ocean_steps.1 = bf16[4,76,1440]{2,1,0:T(8,128)(2,1)} custom-call(bf16[4,76,1440]{2,1,0:T(8,128)(2,1)} %get-tuple-element.11.low_ref, bf16[4,76,1440]{2,1,0:T(8,128)(2,1)} %bitcast.26, bf16[4,76,1440]{2,1,0:T(8,128)(2,1)} %get-tuple-element.12.high_ref, s32[4,1440]{1,0:T(4,128)} %get-tuple-element.13.land_low, s32[4,1440]{1,0:T(4,128)} %land_mid.1, ...), custom_call_target="tpu_custom_call" | custom-call | tf_op jit(solution)/shard_map/ocean_steps/pallas_call | solution.py:396
  95.6 2.9 %copy.32 = bf16[76,4,1440]{2,1,0:T(4,128)(2,1)} copy(bf16[76,4,1440]{2,0,1:T(8,128)(2,1)} %bitcast.27) | data formatting | bytes 1751040
  98.5 0.0 copy-done
  98.5 0.9 copy.45
  (6 shorter events, 0.1 us)
Async XLA Ops:
  0.6 67.6 %copy-start.1 = (bf16[9,128,92]{1,2,0:T(8,128)(2,1)S(1)}, bf16[9,128,92]{1,2,0:T(8,128)(2,1)}, u32[]{:S(2)}) copy-start(bf16[9,128,92]{1,2,0:T(8,128)(2,1)} %param.30) | copy-start | bytes 635908
  6.5 63.3 %copy-start.2 = (bf16[9,76,128]{2,1,0:T(8,128)(2,1)S(1)}, bf16[9,76,128]{2,1,0:T(8,128)(2,1)}, u32[]{:S(2)}) copy-start(bf16[9,76,128]{2,1,0:T(8,128)(2,1)} %param.31) | copy-start | bytes 525316
  68.2 30.2 %copy-start = (bf16[360,1024]{1,0:T(8,128)(2,1)S(1)}, bf16[360,1024]{1,0:T(8,128)(2,1)}, u32[]{:S(2)}) copy-start(bf16[360,1024]{1,0:T(8,128)(2,1)} %get-tuple-element.24) | copy-start | bytes 2211844
